TPU v7x, 256 devices: a whole 4x4x8 slice. The times are simulated.
256 devices in a mesh: blk: 16 (over y, z_lo, core), dp: 16 (over z_hi, x).
Axes of the slice: x: 4, y: 4, z: 8 (z_hi: 4, z_lo: 2; z = z_hi * 2 + z_lo), core: 2. Of those that a mesh axis runs over, the one named last changes fastest.
Arguments:
- queries: bfloat16 [32768, 256], P(('blk', 'dp')), may hold values from -30 to 30, as said below
- pois: bfloat16 [32768, 256], P(('blk', 'dp')), may hold values from -4 to 4, as said below
- query_region: int32 [32768], P(('blk', 'dp')), may hold values from 0 to 63
- block_region: int32 [256], P(('blk', 'dp')), may hold values from 0 to 63
- region_mask: int32 [64, 64], replicated, may hold values from 0 to 1
- positive: int32 [32768], P(('blk', 'dp')), may hold values from 0 to 32767
Outputs:
- loss: float32 [32768], P(('blk', 'dp'))
- query_grad: float32 [32768, 256], P(('blk', 'dp'))
- poi_grad: float32 [32768, 256], P(('blk', 'dp'))
Inputs may be any that keep to these rules, and one draw needn't show every extreme that they name: `queries`: float entries. `pois`: float entries.
All inputs are finite; a program needn't handle non-finite values.
Results may differ from a plain program's by a relative error of at most 0.00185.
Values may be sent and summed in bfloat16 or wider, within the bound.
A program may use at most 64 MiB of HBM per device.

v0:
```python
import math

import jax
import jax.numpy as jnp
from jax import lax
from jax.sharding import PartitionSpec as P

TILE = 128


floor_value = -1e30


def shifted(x, axis, by):
    length = lax.axis_size(axis)
    return lax.ppermute(x, axis, [(i, (i + by) % length) for i in range(length)])


def combined_all(x, axis, combine):
    everything = jax.tree.map(lambda part: lax.all_gather(part, axis), x)
    leading = jax.tree.map(lambda part: part[0], everything)

    def lap(k, so_far):
        return combine(so_far, jax.tree.map(lambda part: part[k], everything))

    return lax.fori_loop(1, lax.axis_size(axis), lap, leading)


def combine_parts(first, second):
    highest = jnp.maximum(first[0], second[0])
    total = first[1] * jnp.exp(first[0] - highest) + second[1] * jnp.exp(second[0] - highest)
    return (highest, total, first[2] + second[2])


def body(queries, pois, query_region, block_region, region_mask, positive):
    group_count = lax.axis_size("dp")
    cycle_count = lax.axis_size("blk")
    cycle_index = lax.axis_index("blk")
    group_index = lax.axis_index("dp")
    slab_rows = pois.shape[0]
    own_rows = queries.shape[0]
    width = queries.shape[1]
    regions = region_mask.shape[0]
    scale = 1.0 / math.sqrt(width)
    group_q = lax.all_gather(queries, "dp", axis=0, tiled=True)
    group_reg, group_pos = (
        lax.all_gather(query_region, "dp", axis=0, tiled=True),
        lax.all_gather(positive, "dp", axis=0, tiled=True),
    )
    block_all = lax.all_gather(block_region, ("blk", "dp"), axis=0, tiled=True)
    group_rows = group_q.shape[0]
    region_ids = jnp.arange(regions, dtype=jnp.int32)
    query_hot = (group_reg[:, None] == region_ids[None, :]).astype(jnp.bfloat16)
    block_hot = (block_all[:, None] == region_ids[None, :]).astype(jnp.bfloat16)
    mask_rows = jnp.dot(
        query_hot, region_mask.astype(jnp.bfloat16), preferred_element_type=jnp.float32
    ).astype(jnp.bfloat16)
    block_open = (
        lax.dot_general(
            mask_rows, block_hot, (((1,), (1,)), ((), ())), preferred_element_type=jnp.float32
        )
        > 0.5
    )
    pos_block = group_pos // TILE

    def anchor_start(anchor):
        return (anchor % cycle_count * group_count + group_index) * slab_rows

    def piece_masks(start, count):
        columns = start + jnp.arange(count, dtype=jnp.int32)
        blocks = columns // TILE
        opened = jnp.take(block_open, blocks, axis=1) | (blocks[None, :] == pos_block[:, None])
        is_pos = columns[None, :] == group_pos[:, None]
        return (opened, is_pos)

    def logits(slab):
        return (
            lax.dot_general(
                group_q, slab, (((1,), (1,)), ((), ())), preferred_element_type=jnp.float32
            )
            * scale
        )

    def forward_piece(state, slab, start):
        opened, is_pos = piece_masks(start, slab.shape[0])
        highest, total, pos_score = state
        scores = logits(slab)
        masked = jnp.where(opened, scores, floor_value)
        new_high = jnp.maximum(highest, jnp.max(masked, axis=1))
        total = total * jnp.exp(highest - new_high) + jnp.sum(
            jnp.where(opened, jnp.exp(scores - new_high[:, None]), 0.0), axis=1
        )
        pos_score = pos_score + jnp.sum(jnp.where(is_pos, scores, 0.0), axis=1)
        return (new_high, total, pos_score)

    def backward_piece(query_acc, slab, start, log_total):
        opened, is_pos = piece_masks(start, slab.shape[0])
        current = query_acc
        scores = logits(slab)
        weights = (
            jnp.where(opened, jnp.exp(scores - log_total[:, None]), 0.0)
            - is_pos.astype(jnp.float32)
        ).astype(jnp.bfloat16)
        current = current + jnp.dot(weights, slab, preferred_element_type=jnp.float32)
        tile_grad = lax.dot_general(
            weights, group_q, (((0,), (0,)), ((), ())), preferred_element_type=jnp.float32
        )
        return (current, tile_grad)

    initial = (
        jnp.full((group_rows,), floor_value, jnp.float32),
        jnp.zeros((group_rows,), jnp.float32),
        jnp.zeros((group_rows,), jnp.float32),
    )
    query_acc = jnp.zeros((group_rows, width), jnp.float32)
    state = forward_piece(initial, pois, anchor_start(cycle_index))

    def forward_step(step, carry):
        slab, current = carry
        slab = shifted(slab, "blk", 1)
        return (slab, forward_piece(current, slab, anchor_start(cycle_index - step)))

    unused, state = lax.fori_loop(1, cycle_count, forward_step, (pois, state))
    highest, total, pos_score = combined_all(state, "dp", combine_parts)
    log_total = highest + jnp.log(total)
    losses = log_total - pos_score
    loss = lax.dynamic_slice_in_dim(losses, group_index * own_rows, own_rows, 0)

    def backward_step(step, carry):
        slab, grads, current = carry
        current, tile_grad = backward_piece(
            current, slab, anchor_start(cycle_index - step), log_total
        )
        grads = grads + tile_grad
        slab = shifted(slab, "blk", 1)
        grads = shifted(grads, "blk", 1)
        return (slab, grads, current)

    start_grads = jnp.zeros((slab_rows, width), jnp.float32)
    unused, poi_sum, query_acc = lax.fori_loop(
        0, cycle_count, backward_step, (pois, start_grads, query_acc)
    )
    query_grad = lax.psum_scatter(query_acc * scale, "dp", scatter_dimension=0, tiled=True)
    return (loss, query_grad, poi_sum * scale)


def solution(mesh):
    in_specs = (
        P(("blk", "dp"), None),
        P(("blk", "dp"), None),
        P(("blk", "dp")),
        P(("blk", "dp")),
        P(),
        P(("blk", "dp")),
    )
    out_specs = (P(("blk", "dp")), P(("blk", "dp"), None), P(("blk", "dp"), None))
    return jax.shard_map(body, mesh=mesh, in_specs=in_specs, out_specs=out_specs, check_vma=False)
```

profile of v0, /device:TPU:1, one launch (start us, length us, event | category | flops | bytes accessed | tf_op | source)
XLA Modules:
  0.0 692.0 jit_solution(1324821323674346143)
XLA Ops:
  8.9 83.4 %all-reduce = s32[256]{0:T(256)S(1)} all-reduce(s32[256]{0:T(256)S(1)} %dynamic-update-slice), channel_id=1, replica_groups=mesh['blk'=16,'dp'=16] {'blk','dp'}, use_global_device_ids=true, to_apply=%add | all-reduce | flops 256 | bytes 2048
  92.3 31.1 %all-gather.3 = s32[16,1,128]{2,1,0:T(1,128)S(1)} all-gather(s32[1,1,128]{2,1,0:T(1,128)} %bitcast.66), channel_id=1, replica_groups=mesh['blk'=16,'dp'=16] {'dp'}, dimensions={0}, use_global_device_ids=true | all-gather | bytes 8704 | tf_op jit(solution)/shard_map/all_gather | solution.py:47
  127.8 32.0 %all-gather.4 = s32[16,1,128]{2,1,0:T(1,128)S(1)} all-gather(s32[1,1,128]{2,1,0:T(1,128)S(1)} %bitcast.67), channel_id=1, replica_groups=mesh['blk'=16,'dp'=16] {'dp'}, dimensions={0}, use_global_device_ids=true | all-gather | bytes 8704 | tf_op jit(solution)/shard_map/all_gather | solution.py:48
  162.3 135.0 %while.60 = (s32[]{:T(128)}, bf16[128,256]{1,0:T(8,128)(2,1)S(1)}, f32[2048]{0:T(1024)S(1)}, f32[2048]{0:T(1024)S(1)}, f32[2048]{0:T(1024)S(1)}, /*index=5*/s32[...) while((s32[]{:T(128)}, bf16[128,256]{1,0:T(8,128)(2,1)S(1)}, ...), condition=%wide.region_7.9_spmd, body=%wide.region_3.8_spmd.sunk | while | flops 138162320 | bytes 4825830 | solution.py:123
  162.3 15.1 %collective-permute-start = (bf16[128,256]{1,0:T(8,128)(2,1)S(1)}, bf16[128,256]{1,0:T(8,128)(2,1)S(1)}, u32[]{:S(2)}, u32[]{:S(2)}) collective-permute-start(bf16[128,256]{1,0:T(8,128)(2,1)S(1)} %get-tuple-element.1101), channel_id=1, source_target_pairs={{0,16},{16,32},{32,48},{48,64},{64,80},{80,96},{96,112},{112,128},... | collective-permute-start | bytes 196616 | tf_op jit(solution)/shard_map/while/body/eval_jaxpr/ppermute | solution.py:16
  191.5 3.5 collective-permute-done
  199.3 4.1 collective-permute-done
  207.6 4.1 collective-permute-done
  215.9 4.1 collective-permute-done
  224.2 4.1 collective-permute-done
  232.5 4.1 collective-permute-done
  240.9 4.1 collective-permute-done
  249.2 4.1 collective-permute-done
  257.5 4.1 collective-permute-done
  265.8 4.1 collective-permute-done
  274.1 4.1 collective-permute-done
  282.5 4.1 collective-permute-done
  290.8 4.1 collective-permute-done
  297.3 31.8 %all-gather = f32[32768]{0:T(1024)S(1)} all-gather(f32[2048]{0:T(1024)S(1)} %get-tuple-element.719), channel_id=2, replica_groups=mesh['blk'=16,'dp'=16] {'dp'}, dimensions={0}, use_global_device_ids=true | all-gather | bytes 139264 | tf_op jit(solution)/shard_map/all_gather | solution.py:20
  329.1 33.3 %all-gather.1 = f32[32768]{0:T(1024)S(1)} all-gather(f32[2048]{0:T(1024)S(1)} %get-tuple-element.720), channel_id=3, replica_groups=mesh['blk'=16,'dp'=16] {'dp'}, dimensions={0}, use_global_device_ids=true | all-gather | bytes 139264 | tf_op jit(solution)/shard_map/all_gather | solution.py:20
  362.4 32.0 %all-gather.2 = f32[32768]{0:T(1024)S(1)} all-gather(f32[2048]{0:T(1024)S(1)} %get-tuple-element.721), channel_id=4, replica_groups=mesh['blk'=16,'dp'=16] {'dp'}, dimensions={0}, use_global_device_ids=true | all-gather | bytes 139264 | tf_op jit(solution)/shard_map/all_gather | solution.py:20
  396.7 200.7 %while.62 = (s32[]{:T(128)}, bf16[128,256]{1,0:T(8,128)(2,1)S(1)}, f32[128,256]{1,0:T(8,128)S(1)}, f32[2048,256]{1,0:T(8,128)S(1)}, s32[]{:T(128)}, /*index=5*/s...) while((s32[]{:T(128)}, bf16[128,256]{1,0:T(8,128)(2,1)S(1)}, ...), condition=%wide.region_11.13_spmd.clone, body=%wide.region_10.12_spmd.clone.sunk | while | flops 406362368 | bytes 14713012 | solution.py:140
  396.7 19.6 %collective-permute-start.1 = (bf16[128,256]{1,0:T(8,128)(2,1)S(1)}, bf16[128,256]{1,0:T(8,128)(2,1)S(1)}, u32[]{:S(2)}, u32[]{:S(2)}) collective-permute-start(bf16[128,256]{1,0:T(8,128)(2,1)S(1)} %copy.52), channel_id=1, source_target_pairs={{0,16},{16,32},{32,48},{48,64},{64,80},{80,96},{96,112},{112,128},... | collective-permute-start | bytes 196616 | tf_op jit(solution)/shard_map/while/body/eval_jaxpr/ppermute | solution.py:16
  418.4 2.2 fusion.39
  421.7 2.5 collective-permute-done.1
  424.3 4.8 collective-permute-done.2
  431.2 2.2 fusion.39
  435.5 4.8 collective-permute-done.2
  446.7 4.8 collective-permute-done.2
  453.6 2.2 fusion.39
  457.9 4.8 collective-permute-done.2
  469.2 4.8 collective-permute-done.2
  476.1 2.2 fusion.39
  480.4 4.8 collective-permute-done.2
  487.3 2.2 fusion.39
  491.6 4.8 collective-permute-done.2
  502.8 4.8 collective-permute-done.2
  514.0 4.8 collective-permute-done.2
  525.2 4.8 collective-permute-done.2
  536.5 4.8 collective-permute-done.2
  547.7 4.8 collective-permute-done.2
  558.9 4.8 collective-permute-done.2
  570.1 4.8 collective-permute-done.2
  577.0 2.2 fusion.39
  581.3 4.8 collective-permute-done.2
  588.2 2.2 fusion.39
  592.5 4.8 collective-permute-done.2
  600.8 84.4 %reduce-scatter.2.cloned.1.call-done = f32[128,256]{1,0:T(8,128)} async-done(((f32[2048,256]{1,0:T(8,128)}), f32[128,256]{1,0:T(8,128)}) %reduce-scatter.2.cloned.1.call-update) | async-done | bytes 131088 | tf_op jit(solution)/shard_map/reduce_scatter | solution.py:143
  (525 shorter events, 164.7 us)
Async XLA Ops:
  7.2 152.7 %all-gather.7.cloned.1.call-start = ((), (), s32[]{:S(2)}) async-start(), calls=%async_computation.1 | async-start | bytes 1114112 | tf_op jit(solution)/shard_map/all_gather | solution.py:45
  8.1 677.1 %reduce-scatter.2.cloned.1.call-start = ((), (), s32[]{:S(2)}) async-start(), calls=%async_computation.2 | async-start | bytes 2228224 | tf_op jit(solution)/shard_map/reduce_scatter | solution.py:143
  162.3 16.8 %collective-permute-start = (bf16[128,256]{1,0:T(8,128)(2,1)S(1)}, bf16[128,256]{1,0:T(8,128)(2,1)S(1)}, u32[]{:S(2)}, u32[]{:S(2)}) collective-permute-start(bf16[128,256]{1,0:T(8,128)(2,1)S(1)} %get-tuple-element.1101), channel_id=1, source_target_pairs={{0,16},{16,32},{32,48},{48,64},{64,80},{80,96},{96,112},{112,128},... | collective-permute-start | bytes 196616 | tf_op jit(solution)/shard_map/while/body/eval_jaxpr/ppermute | solution.py:16
  189.1 5.9 collective-permute-start
  197.4 5.9 collective-permute-start
  205.8 5.9 collective-permute-start
  214.1 5.9 collective-permute-start
  222.4 5.9 collective-permute-start
  230.7 5.9 collective-permute-start
  239.0 5.9 collective-permute-start
  247.4 5.9 collective-permute-start
  255.7 5.9 collective-permute-start
  264.0 5.9 collective-permute-start
  272.3 5.9 collective-permute-start
  280.6 5.9 collective-permute-start
  289.0 5.9 collective-permute-start
  396.7 27.6 %collective-permute-start.1 = (bf16[128,256]{1,0:T(8,128)(2,1)S(1)}, bf16[128,256]{1,0:T(8,128)(2,1)S(1)}, u32[]{:S(2)}, u32[]{:S(2)}) collective-permute-start(bf16[128,256]{1,0:T(8,128)(2,1)S(1)} %copy.52), channel_id=1, source_target_pairs={{0,16},{16,32},{32,48},{48,64},{64,80},{80,96},{96,112},{112,128},... | collective-permute-start | bytes 196616 | tf_op jit(solution)/shard_map/while/body/eval_jaxpr/ppermute | solution.py:16
  420.9 8.2 %collective-permute-start.2 = (f32[128,256]{1,0:T(8,128)S(1)}, f32[128,256]{1,0:T(8,128)S(1)}, u32[]{:S(2)}, u32[]{:S(2)}) collective-permute-start(f32[128,256]{1,0:T(8,128)S(1)} %convolution_add_fusion.4), channel_id=1, source_target_pairs={{0,16},{16,32},{32,48},{48,64},{64,80},{80,96},{96,112},{112,128},... | collective-permute-start | bytes 393224 | tf_op jit(solution)/shard_map/while/body/eval_jaxpr/ppermute | solution.py:16
  429.1 6.4 collective-permute-start.1
  433.7 6.6 collective-permute-start.2
  440.3 6.4 collective-permute-start.1
  445.0 6.6 collective-permute-start.2
  451.5 6.4 collective-permute-start.1
  456.2 6.6 collective-permute-start.2
  462.8 6.4 collective-permute-start.1
  467.4 6.6 collective-permute-start.2
  474.0 6.4 collective-permute-start.1
  478.6 6.6 collective-permute-start.2
  485.2 6.4 collective-permute-start.1
  489.8 6.6 collective-permute-start.2
  496.4 6.4 collective-permute-start.1
  501.0 6.6 collective-permute-start.2
  507.6 6.4 collective-permute-start.1
  512.3 6.6 collective-permute-start.2
  518.8 6.4 collective-permute-start.1
  523.5 6.6 collective-permute-start.2
  530.1 6.4 collective-permute-start.1
  534.7 6.6 collective-permute-start.2
  541.3 6.4 collective-permute-start.1
  545.9 6.6 collective-permute-start.2
  552.5 6.4 collective-permute-start.1
  557.1 6.6 collective-permute-start.2
  563.7 6.4 collective-permute-start.1
  568.3 6.6 collective-permute-start.2
  574.9 6.4 collective-permute-start.1
  579.6 6.6 collective-permute-start.2
  586.1 6.4 collective-permute-start.1
  590.8 6.6 collective-permute-start.2
  (19 other events, 43.5 us)
Sparse Core Ops, SparseCore 0:
  10.4 56.3 all-gather.6
  599.0 86.1 reduce-scatter.1
where the time goes:
time: 694 us; the launch traced here: 692 us
  blocking collectives  244 us (35%)
  waiting for transfers between devices  232 us (33%)
  matrix products  81.5 us (12%)
  local copies, waits for them, and re-layouts  60.6 us (9%)
  starting transfers between devices  39.9 us (6%)
  other arithmetic  15.1 us (2%)
  between operations  14.9 us (2%)
    ppermute x47, waiting for transfers between devices, shifted(): lax.ppermute(x, axis, [(i, (i + by) % length) for i in range(length)])  147 us
    all_gather x3, blocking collectives, combined_all(): everything = jax.tree.map(lambda part: lax.all_gather(part, axis), x)  97 us
    reduce_scatter x1, waiting for transfers between devices, body(): lax.psum_scatter(query_acc * scale, 'dp', scatter_dimension=0, tiled=True)  84.4 us
    unnamed x1, blocking collectives  83.4 us
    dot_general x32, matrix products, logits(): lax.dot_general(group_q, slab, (((1,), (1,)), ((), ())), preferred_elemen...  63.1 us
    gather x48, local copies, waits for them, and re-layouts, piece_masks(): jnp.take(block_open, blocks, axis=1)  57.7 us
    ppermute x47, starting transfers between devices, shifted(): lax.ppermute(x, axis, [(i, (i + by) % length) for i in range(length)])  39.8 us
    all_gather x1, blocking collectives, body(): lax.all_gather(positive, 'dp', axis=0, tiled=True)  32 us
  transfers between devices with their start and end apart: 49, of which 47 were waited for; matrix products, arithmetic and copies ran while one was open for 17% of the time, Pallas kernels for 0%

commit v1 on v0

v1 whole, which is shorter than its diff:
```python
import math

import jax
import jax.numpy as jnp
from jax import lax
from jax.experimental import pallas as pl
from jax.experimental.pallas import tpu as pltpu
from jax.sharding import PartitionSpec as P

MESH = pl.DeviceIdType.MESH
TILE = 128
EXT = 144
NX, NY, NZ = 4, 4, 8
PLANE = NX * NY
DZ = (0, 1, 7, 2, 6, 3, 5, 4)
MIRROR = tuple(DZ.index((NZ - d) % NZ) for d in DZ)
CLOSED = -1e30
FLOOR = -1e29
NT = (((1,), (1,)), ((), ()))
f32, bf16 = jnp.float32, jnp.bfloat16


def kernel(
    q_ref, p_ref, reg_ref, pos_ref, breg_ref, mask_ref,
    loss_ref, qg_ref, pg_ref,
    qall, pall, pt, hot, posf, bias, es, wts, mk, lk, ps, st, nrm, psr, acc,
    own, cbuf, crecv, zsend, zrecv, qsend, qrecv,
    q_ss, q_rs, p_ss, p_rs, f_ss, f_rs, n_ss, n_rs, s_ss, s_rs,
    c_ss, c_rs, z_ss, z_rs, g_ss, g_rs,
):
    blk = lax.axis_index("blk")
    dp = lax.axis_index("dp")
    core = blk % 2
    y = blk // 4
    x = dp % NX
    z = (dp // NX) * 2 + (blk // 2) % 2
    width = q_ref.shape[1]
    rows = q_ref.shape[0]
    nq = PLANE * rows
    scale = 1.0 / math.sqrt(width)

    def device(xx, yy, zz, cc):
        return (yy * 4 + (zz % 2) * 2 + cc, (zz // 2) * NX + xx)

    def plane_peer(dx, dy):
        return device((x + dx) % NX, (y + dy) % NY, z, core)

    def z_peer(dz):
        return device(x, y, (z + dz) % NZ, core)

    sibling = device(x, y, z, 1 - core)

    def remote(src, dst, ss, rs, dev):
        return pltpu.make_async_remote_copy(
            src_ref=src, dst_ref=dst, send_sem=ss, recv_sem=rs, device_id=dev, device_id_type=MESH
        )

    def back(slot):
        return ((NY - slot // NX) % NY) * NX + (NX - slot % NX) % NX

    barrier = pltpu.get_barrier_semaphore()
    for slot in range(1, PLANE):
        pl.semaphore_signal(barrier, inc=1, device_id=plane_peer(slot % NX, slot // NX), device_id_type=MESH)
    for dz in range(1, NZ):
        pl.semaphore_signal(barrier, inc=1, device_id=z_peer(dz), device_id_type=MESH)
    pl.semaphore_signal(barrier, inc=1, device_id=sibling, device_id_type=MESH)

    qall[0, :rows, :] = q_ref[...]
    pall[0, :rows, :] = p_ref[...]
    row = lax.broadcasted_iota(jnp.int32, (16, rows), 0)
    pos = pos_ref[...]
    small = jnp.where(row == 0, reg_ref[...], jnp.where(row == 1, pos // TILE, pos % TILE)).astype(f32)
    small = small.astype(bf16)
    qall[0, rows:, :rows] = small
    qall[0, rows:, rows:] = small
    pall[0, rows:, :] = jnp.full((16, width), breg_ref[0], jnp.int32).astype(f32).astype(bf16)

    pl.semaphore_wait(barrier, PLANE + NZ - 1)

    def q_copy(slot):
        return remote(qall.at[0], qall.at[back(slot)], q_ss.at[slot], q_rs.at[back(slot)],
                      plane_peer(slot % NX, slot // NX))

    def p_copy(t):
        return remote(pall.at[0], pall.at[2 * MIRROR[t]], p_ss.at[t], p_rs.at[MIRROR[t]], z_peer(DZ[t]))

    def f_copy(t):
        return remote(pall.at[2 * t], pall.at[2 * t + 1], f_ss.at[t], f_rs.at[t], sibling)

    f_copy(0).start()
    for t in range(1, NZ):
        p_copy(t).start()
    for slot in range(1, PLANE):
        q_copy(slot).start()

    ps[...] = jnp.zeros_like(ps)
    region_mask = mask_ref[...].astype(f32).astype(bf16)
    regions = region_mask.shape[0]

    def take_query_small(slot):
        extra = qall[slot, rows:, :rows].astype(f32)
        lanes = slice(slot * rows, (slot + 1) * rows)
        region_ids = lax.broadcasted_iota(jnp.int32, (regions, rows), 0).astype(f32)
        hot[:, lanes] = (region_ids == extra[0:1]).astype(f32).astype(bf16)
        posf[0:8, lanes] = jnp.broadcast_to(extra[1:2], (8, rows))
        posf[8:16, lanes] = jnp.broadcast_to(extra[2:3] + extra[1:2] * TILE, (8, rows))

    take_query_small(0)
    for slot in range(1, PLANE):
        q_copy(back(slot)).wait_recv()
        take_query_small(slot)

    lane64 = lax.broadcasted_iota(jnp.int32, (8, regions), 1).astype(f32)
    iota = lax.broadcasted_iota(jnp.int32, (rows, 256), 0).astype(f32)
    chunks = nq // 256
    log2e_scale = scale / math.log(2.0)

    def block_ids(t):
        zz = (z + DZ[t]) % NZ
        ids = []
        for cc in (core, 1 - core):
            b, d = device(x, y, zz, cc)
            ids.append((b * 16 + d).astype(f32))
        return ids

    def group_sum(v):
        return jnp.sum(v.reshape(v.shape[0] // 8, 8, v.shape[1]), axis=0)

    for t in range(NZ):
        if t > 0:
            p_copy(MIRROR[t]).wait_recv()
            f_copy(t).start()
        f_copy(t).wait_recv()
        ids = block_ids(t)
        hots = [
            (lane64 == pall[2 * t + h, rows:rows + 8, :regions].astype(f32)).astype(f32)
            for h in range(2)
        ]
        picked = lax.dot_general(
            jnp.concatenate(hots, axis=0).astype(bf16), region_mask, NT, preferred_element_type=f32
        ).astype(bf16)
        opened = jnp.dot(picked, hot[...], preferred_element_type=f32)
        for h in range(2):
            part = (opened[8 * h:8 * h + 8] > 0.5) | (posf[0:8, :] == ids[h])
            bias[8 * h:8 * h + 8, :] = jnp.where(part, 0.0, CLOSED)
        pt[:, t * 256:(t + 1) * 256] = pall[2 * t:2 * t + 2, :rows, :].reshape(256, width).T

        def score_chunk(g, carry, t=t, ids=ids):
            lanes = pl.ds(pl.multiple_of(g * 256, 256), 256)
            pair = pall[2 * t:2 * t + 2, :rows, :].reshape(256, width)
            qg = qall[pl.ds(2 * g, 2), :rows, :].reshape(256, width)
            s = lax.dot_general(pair, qg, NT, preferred_element_type=f32)
            target = posf[8:9, lanes]
            high = None
            found = ps[:, lanes]
            shifted = []
            for h in range(2):
                part = s[h * rows:(h + 1) * rows]
                found += group_sum(jnp.where(iota == target - ids[h] * TILE, part, 0.0))
                part = part.reshape(16, 8, 256) * log2e_scale + bias[8 * h:8 * h + 8, lanes][None]
                shifted.append(part)
                top = jnp.max(part, axis=0)
                high = top if high is None else jnp.maximum(high, top)
            ps[:, lanes] = found
            high = jnp.maximum(jnp.max(high, axis=0, keepdims=True), FLOOR)
            high = jnp.broadcast_to(high, (8, 256))
            mk[t, :, lanes] = high
            total = jnp.zeros((8, 256), f32)
            for h in range(2):
                e = jnp.exp2(shifted[h] - high[None])
                total += jnp.sum(e, axis=0)
                es[t, h * rows:(h + 1) * rows, lanes] = e.reshape(rows, 256)
            lk[t, :, lanes] = total
            return carry

        lax.fori_loop(0, chunks, score_chunk, 0)

    high = mk[0]
    for t in range(1, NZ):
        high = jnp.maximum(high, mk[t])
    total = jnp.zeros((8, nq), f32)
    for t in range(NZ):
        total += lk[t] * jnp.exp2(mk[t] - high)
    st[0:1, :] = high[0:1]
    st[1:2, :] = jnp.sum(total, axis=0, keepdims=True)

    def n_copy(slot):
        return remote(st, nrm.at[back(slot)], n_ss.at[slot], n_rs.at[back(slot)],
                      plane_peer(slot % NX, slot // NX))

    def s_copy(slot):
        return remote(ps.at[:, slot * rows:(slot + 1) * rows], psr.at[back(slot)], s_ss.at[slot],
                      s_rs.at[back(slot)], plane_peer(slot % NX, slot // NX))

    for slot in range(1, PLANE):
        n_copy(slot).start()
    for slot in range(1, PLANE):
        s_copy(slot).start()

    parts = [st[...]]
    for slot in range(1, PLANE):
        n_copy(back(slot)).wait_recv()
        sx, sy = slot % NX, slot // NX
        pieces = []
        for mine in range(PLANE):
            theirs = ((mine // NX - sy) % NY) * NX + (mine % NX - sx) % NX
            pieces.append(nrm[slot, :, theirs * rows:(theirs + 1) * rows])
        parts.append(jnp.concatenate(pieces, axis=1))
    high = parts[0][0:1]
    for part in parts[1:]:
        high = jnp.maximum(high, part[0:1])
    total = jnp.zeros((1, nq), f32)
    for part in parts:
        total += part[1:2] * jnp.exp2(part[0:1] - high)
    log_total = high + jnp.log2(total)
    for t in range(NZ):
        mk[t] = jnp.exp2(mk[t] - log_total)
    lsum = log_total[:, :rows] * math.log(2.0)

    def c_copy(t):
        return remote(cbuf.at[t], crecv.at[t], c_ss.at[t], c_rs.at[t], sibling)

    def z_copy(t):
        return remote(zsend.at[t], zrecv.at[MIRROR[t]], z_ss.at[t], z_rs.at[MIRROR[t]], z_peer(DZ[t]))

    def combine(t):
        c_copy(t).wait_recv()
        zsend[t] = own[t] + crecv[t]
        if t > 0:
            z_copy(t).start()

    order = tuple(range(NZ - 1, -1, -1))
    for number, t in enumerate(order):
        ids = block_ids(t)

        acc[...] = jnp.zeros_like(acc)

        def weight_chunk(g, carry, t=t, ids=ids):
            lanes = pl.ds(pl.multiple_of(g * 256, 256), 256)
            target = posf[8:9, lanes]
            factor = mk[t, :, lanes]
            halves = []
            for h in range(2):
                e = es[t, h * rows:(h + 1) * rows, lanes].reshape(16, 8, 256) * factor[None]
                e = e.reshape(rows, 256)
                halves.append(jnp.where(iota == target - ids[h] * TILE, e - 1.0, e).astype(bf16))
            w = jnp.concatenate(halves, axis=0)
            wts[t * 256:(t + 1) * 256, lanes] = w
            qg = qall[pl.ds(2 * g, 2), :rows, :].reshape(256, width)
            acc[...] += jnp.dot(w, qg, preferred_element_type=f32)
            return carry

        lax.fori_loop(0, chunks, weight_chunk, 0)
        own[t] = acc[:rows]
        cbuf[t] = acc[rows:]
        c_copy(t).start()
        if number > 0:
            combine(order[number - 1])
    combine(order[-1])

    def g_copy(slot):
        return remote(qsend.at[slot], qrecv.at[back(slot)], g_ss.at[slot], g_rs.at[back(slot)],
                      plane_peer(slot % NX, slot // NX))

    def query_chunk(g):
        lanes = pl.ds(pl.multiple_of(g * 256, 256), 256)
        grad = jnp.dot(pt[...], wts[:, lanes], preferred_element_type=f32)
        qsend[2 * g] = grad[:, :rows]
        qsend[2 * g + 1] = grad[:, rows:]

    def query_step(g, carry):
        query_chunk(g)
        g_copy(2 * g).start()
        g_copy(2 * g + 1).start()
        return carry

    lax.fori_loop(1, chunks, query_step, 0)
    query_chunk(0)
    g_copy(1).start()

    found = ps[:, :rows]
    for slot in range(1, PLANE):
        s_copy(back(slot)).wait_recv()
        found += psr[slot]
    loss_ref[...] = lsum - jnp.sum(found, axis=0, keepdims=True) * scale

    grads = zsend[0]
    for t in range(1, NZ):
        z_copy(MIRROR[t]).wait_recv()
        grads += zrecv[t]
    pg_ref[...] = grads * scale

    grads = qsend[0]
    for slot in range(1, PLANE):
        g_copy(back(slot)).wait_recv()
        grads += qrecv[slot]
    qg_ref[...] = (grads * scale).T

    for t in range(NZ):
        f_copy(t).wait_send()
        c_copy(t).wait_send()
    for t in range(1, NZ):
        p_copy(t).wait_send()
        z_copy(t).wait_send()
    for slot in range(1, PLANE):
        q_copy(slot).wait_send()
        n_copy(slot).wait_send()
        s_copy(slot).wait_send()
        g_copy(slot).wait_send()


def body(queries, pois, query_region, block_region, region_mask, positive):
    rows, width = queries.shape
    regions = region_mask.shape[0]
    nq = PLANE * rows
    npoi = 2 * NZ * rows
    vmem = pl.BlockSpec(memory_space=pltpu.VMEM)
    dma = pltpu.SemaphoreType.DMA
    loss, query_grad, poi_grad = pl.pallas_call(
        kernel,
        out_shape=(
            jax.ShapeDtypeStruct((1, rows), f32),
            jax.ShapeDtypeStruct((rows, width), f32),
            jax.ShapeDtypeStruct((rows, width), f32),
        ),
        in_specs=[vmem, vmem, vmem, vmem, pl.BlockSpec(memory_space=pltpu.SMEM), vmem],
        out_specs=(vmem, vmem, vmem),
        scratch_shapes=[
            pltpu.VMEM((PLANE, EXT, width), bf16),
            pltpu.VMEM((2 * NZ, EXT, width), bf16),
            pltpu.VMEM((width, npoi), bf16),
            pltpu.VMEM((regions, nq), bf16),
            pltpu.VMEM((16, nq), f32),
            pltpu.VMEM((16, nq), f32),
            pltpu.VMEM((NZ, 2 * rows, nq), f32),
            pltpu.VMEM((npoi, nq), bf16),
            pltpu.VMEM((NZ, 8, nq), f32),
            pltpu.VMEM((NZ, 8, nq), f32),
            pltpu.VMEM((8, nq), f32),
            pltpu.VMEM((2, nq), f32),
            pltpu.VMEM((PLANE, 2, nq), f32),
            pltpu.VMEM((PLANE, 8, rows), f32),
            pltpu.VMEM((2 * rows, width), f32),
            pltpu.VMEM((NZ, rows, width), f32),
            pltpu.VMEM((NZ, rows, width), f32),
            pltpu.VMEM((NZ, rows, width), f32),
            pltpu.VMEM((NZ, rows, width), f32),
            pltpu.VMEM((NZ, rows, width), f32),
            pltpu.VMEM((PLANE, width, rows), f32),
            pltpu.VMEM((PLANE, width, rows), f32),
            dma((PLANE,)), dma((PLANE,)), dma((NZ,)), dma((NZ,)), dma((NZ,)), dma((NZ,)),
            dma((PLANE,)), dma((PLANE,)), dma((PLANE,)), dma((PLANE,)),
            dma((NZ,)), dma((NZ,)), dma((NZ,)), dma((NZ,)), dma((PLANE,)), dma((PLANE,)),
        ],
        compiler_params=pltpu.CompilerParams(
            collective_id=0, has_side_effects=True, vmem_limit_bytes=56 * 2**20
        ),
    )(
        queries, pois, query_region.reshape(1, rows), positive.reshape(1, rows), block_region, region_mask
    )
    return (loss.reshape(rows), query_grad, poi_grad)


def solution(mesh):
    in_specs = (
        P(("blk", "dp"), None),
        P(("blk", "dp"), None),
        P(("blk", "dp")),
        P(("blk", "dp")),
        P(),
        P(("blk", "dp")),
    )
    out_specs = (P(("blk", "dp")), P(("blk", "dp"), None), P(("blk", "dp"), None))
    return jax.shard_map(body, mesh=mesh, in_specs=in_specs, out_specs=out_specs, check_vma=False)
```

time: 694 us -> 116 us (0.17)
  blocking collectives: 244 us -> 0 us
  waiting for transfers between devices: 232 us -> 0 us
  Pallas kernels: 0 us -> 111 us
  matrix products: 81.5 us -> 0 us
  local copies, waits for them, and re-layouts: 60.6 us -> 3.44 us
  starting transfers between devices: 39.9 us -> 0 us
  other arithmetic: 15.1 us -> 0 us
  between operations: 14.9 us -> 1.3 us
    all_gather x5 -> x0, blocking collectives: 160 us -> none  [the longest x3 97 us: combined_all(): everything = jax.tree.map(lambda part: lax.all_gather(part, axis), x)]
    ppermute x47 -> x0, waiting for transfers between devices: 147 us -> none  [shifted(): lax.ppermute(x, axis, [(i, (i + by) % length) for i in range(length)])]
    pallas_call x0 -> x1, Pallas kernels: none -> 111 us  [body(): pl.pallas_call(kernel, out_shape=(jax.ShapeDtypeStruct((1, rows), f32), j...]
    reduce_scatter x1 -> x0, waiting for transfers between devices: 84.4 us -> none  [body(): lax.psum_scatter(query_acc * scale, 'dp', scatter_dimension=0, tiled=True)]
    unnamed x1 -> x0, blocking collectives: 83.4 us -> none
    dot_general x65 -> x0, matrix products: 81.5 us -> none  [the longest x32 63.1 us: logits(): lax.dot_general(group_q, slab, (((1,), (1,)), ((), ())), preferred_elemen...]
    gather x48 -> x0, local copies, waits for them, and re-layouts: 57.7 us -> none  [piece_masks(): jnp.take(block_open, blocks, axis=1)]
    ppermute x47 -> x0, starting transfers between devices: 39.8 us -> none  [shifted(): lax.ppermute(x, axis, [(i, (i + by) % length) for i in range(length)])]
  transfers between devices with their start and end apart: 49 -> 0, of which waited for: 47 -> 0; matrix products, arithmetic and copies ran while one was open for 17% -> 0% of each run, Pallas kernels for 0% -> 0%
where the time goes in v1:
time: 116 us
  Pallas kernels  111 us (96%)
  local copies, waits for them, and re-layouts  3.44 us (3%)
  between operations  1.3 us (1%)
    pallas_call x1, Pallas kernels, body(): pl.pallas_call(kernel, out_shape=(jax.ShapeDtypeStruct((1, rows), f32), j...  111 us
    unnamed x7, local copies, waits for them, and re-layouts  3.44 us

profile of v1, /device:TPU:1, one launch (start us, length us, event | category | flops | bytes accessed | tf_op | source)
XLA Modules:
  0.0 116.1 jit_solution(3713355717238942449)
XLA Ops:
  1.3 111.4 %shard_map.85 = (f32[1,128]{1,0:T(1,128)}, f32[128,256]{1,0:T(8,128)}, f32[128,256]{1,0:T(8,128)}) custom-call(bf16[128,256]{1,0:T(8,128)(2,1)} %q_ref.1, bf16[128,256]{1,0:T(8,128)(2,1)} %p_ref.1, s32[1,128]{1,0:T(1,128)} %bitcast.3, s32[1,128]{1,0:T(1,128)} %bitcast.4, s32[1]{0:T(128)S(6)} %copy.12.breg_ref, s32[64,64]{1,0:T(8,128)} %mask_ref.1), custom_call_target="tpu_custom_call" | custom-call | tf_op jit(solution)/shard_map/pallas_call | solution.py:319
  112.7 0.0 copy-start.1
  112.7 0.7 copy-done.1
  113.3 0.5 copy.13
  113.8 0.0 copy-start
  113.8 1.6 %copy.14 = f32[128,256]{1,0:T(8,128)} copy(f32[128,256]{1,0:T(8,128)} %get-tuple-element.13) | data formatting | bytes 262144
  115.4 0.0 copy-done
  115.4 0.7 copy.15
Async XLA Ops:
  112.7 0.7 copy-start.1
  113.8 1.6 %copy-start = (f32[128,256]{1,0:T(8,128)S(1)}, f32[128,256]{1,0:T(8,128)}, u32[]{:S(2)}) copy-start(f32[128,256]{1,0:T(8,128)} %get-tuple-element.14) | copy-start | bytes 393220

commit v2 on v1

v2 whole, which is shorter than its diff:
```python
import math

import jax
import jax.numpy as jnp
from jax import lax
from jax.experimental import pallas as pl
from jax.experimental.pallas import tpu as pltpu
from jax.sharding import PartitionSpec as P

MESH = pl.DeviceIdType.MESH
TILE = 128
EXT = 144
NX, NY, NZ = 4, 4, 8
PLANE = NX * NY
DZ = (0, 1, 7, 2, 6, 3, 5, 4)
ZBACK = tuple(DZ.index((NZ - d) % NZ) for d in DZ)
DXY = (
    (0, 0), (1, 0), (3, 0), (0, 1), (0, 3), (1, 1), (3, 3), (1, 3),
    (3, 1), (2, 0), (0, 2), (2, 1), (2, 3), (1, 2), (3, 2), (2, 2),
)
BACK = tuple(DXY.index(((NX - a) % NX, (NY - b) % NY)) for a, b in DXY)
CLOSED = -1e30
FLOOR = -1e29
TOP = 32767.0
NT = (((1,), (1,)), ((), ()))
f32, bf16 = jnp.float32, jnp.bfloat16


def quantized(v):
    top = jnp.max(jnp.abs(v.reshape(v.shape[0] // 8, 8, v.shape[1])), axis=0)
    top = jnp.max(top, axis=0, keepdims=True)
    step = jnp.where(top > 0.0, TOP / top, 0.0)
    return jnp.round(v * step).astype(jnp.int32).astype(jnp.int16), top * (1.0 / TOP)


def kernel(
    q_ref, p_ref, reg_ref, pos_ref, breg_ref, mask_ref,
    loss_ref, qg_ref, pg_ref,
    qall, pall, pt, hot, pick, tg, bias, es, wts, mk, lk, ps, st, nrm, side, sidr,
    own, cbuf, crecv, zown, zsend, zrecv, zstep, zstepr, qown, qsend, qrecv,
    q_ss, q_rs, p_ss, p_rs, f_ss, f_rs, n_ss, n_rs, s_ss, s_rs,
    c_ss, c_rs, z_ss, z_rs, y_ss, y_rs, g_ss, g_rs,
):
    blk = lax.axis_index("blk")
    dp = lax.axis_index("dp")
    core = blk % 2
    y = blk // 4
    x = dp % NX
    z = (dp // NX) * 2 + (blk // 2) % 2
    width = q_ref.shape[1]
    rows = q_ref.shape[0]
    nq = PLANE * rows
    scale = 1.0 / math.sqrt(width)

    def device(xx, yy, zz, cc):
        return (yy * 4 + (zz % 2) * 2 + cc, (zz // 2) * NX + xx)

    def plane_peer(slot):
        return device((x + DXY[slot][0]) % NX, (y + DXY[slot][1]) % NY, z, core)

    def z_peer(t):
        return device(x, y, (z + DZ[t]) % NZ, core)

    sibling = device(x, y, z, 1 - core)

    def remote(src, dst, ss, rs, dev):
        return pltpu.make_async_remote_copy(
            src_ref=src, dst_ref=dst, send_sem=ss, recv_sem=rs, device_id=dev, device_id_type=MESH
        )

    barrier = pltpu.get_barrier_semaphore()
    for slot in range(1, PLANE):
        pl.semaphore_signal(barrier, inc=1, device_id=plane_peer(slot), device_id_type=MESH)
    for t in range(1, NZ):
        pl.semaphore_signal(barrier, inc=1, device_id=z_peer(t), device_id_type=MESH)
    pl.semaphore_signal(barrier, inc=1, device_id=sibling, device_id_type=MESH)

    qall[0, :rows, :] = q_ref[...]
    pall[0, :rows, :] = p_ref[...]
    row = lax.broadcasted_iota(jnp.int32, (16, rows), 0)
    pos = pos_ref[...]
    small = jnp.where(row == 0, reg_ref[...], jnp.where(row == 1, pos // TILE, pos % TILE)).astype(f32)
    small = small.astype(bf16)
    qall[0, rows:, :rows] = small
    qall[0, rows:, rows:] = small
    pall[0, rows:, :] = jnp.full((16, width), breg_ref[0], jnp.int32).astype(f32).astype(bf16)

    pl.semaphore_wait(barrier, PLANE + NZ - 1)

    def q_copy(slot):
        return remote(qall.at[0], qall.at[BACK[slot]], q_ss.at[slot], q_rs.at[BACK[slot]], plane_peer(slot))

    def p_copy(t):
        return remote(pall.at[0], pall.at[2 * ZBACK[t]], p_ss.at[t], p_rs.at[ZBACK[t]], z_peer(t))

    def f_copy(t):
        return remote(pall.at[2 * t], pall.at[2 * t + 1], f_ss.at[t], f_rs.at[t], sibling)

    f_copy(0).start()
    for slot in range(1, PLANE):
        q_copy(slot).start()
        if slot < NZ:
            p_copy(slot).start()

    ps[...] = jnp.zeros_like(ps)
    region_mask = mask_ref[...].astype(f32).astype(bf16)
    regions = region_mask.shape[0]
    region_ids = lax.broadcasted_iota(jnp.int32, (regions, rows), 0).astype(f32)
    lane_ids = lax.broadcasted_iota(jnp.int32, (8, regions), 1).astype(f32)
    within = lax.broadcasted_iota(jnp.int32, (2 * rows, 256), 0) % rows
    within = within.astype(f32).reshape(2, 16, 8, 256)
    starts = []
    for t in range(NZ):
        for cc in (core, 1 - core):
            b, d = device(x, y, (z + DZ[t]) % NZ, cc)
            starts.append(((b * 16 + d) * TILE).astype(f32))

    def take_queries(slot):
        extra = qall[slot, rows:, :rows].astype(f32)
        lanes = slice(slot * rows, (slot + 1) * rows)
        hot[:, lanes] = (region_ids == extra[0:1]).astype(f32).astype(bf16)
        target = jnp.broadcast_to(extra[1:2] * TILE + extra[2:3], (8, rows))
        for k, start in enumerate(starts):
            tg[k // 2, 8 * (k % 2):8 * (k % 2) + 8, lanes] = target - start

    def take_pair(t):
        pair = pall[2 * t:2 * t + 2, :rows, :].reshape(256, width)
        pt[:, t * 256:(t + 1) * 256] = pair.T
        hots = [
            (lane_ids == pall[2 * t + h, rows:rows + 8, :regions].astype(f32)).astype(f32)
            for h in range(2)
        ]
        pick[16 * t:16 * t + 16, :] = lax.dot_general(
            jnp.concatenate(hots, axis=0).astype(bf16), region_mask, NT, preferred_element_type=f32
        ).astype(bf16)

    def set_bias(first, last, lanes):
        opened = jnp.dot(pick[16 * first:16 * last, :], hot[:, lanes], preferred_element_type=f32)
        for t in range(first, last):
            at = tg[t, :, lanes]
            part = (opened[16 * (t - first):16 * (t - first) + 16] > 0.5) | ((at >= 0.0) & (at < TILE))
            bias[t, :, lanes] = jnp.where(part, 0.0, CLOSED)

    log2e_scale = scale / math.log(2.0)

    def score_tile(t, g):
        lanes = slice(g * 256, (g + 1) * 256)
        pair = pall[2 * t:2 * t + 2, :rows, :].reshape(256, width)
        qg = qall[2 * g:2 * g + 2, :rows, :].reshape(256, width)
        s = lax.dot_general(pair, qg, NT, preferred_element_type=f32).reshape(2, 16, 8, 256)
        target = tg[t, :, lanes].reshape(2, 1, 8, 256)
        ps[:, lanes] += jnp.sum(jnp.where(within == target, s, 0.0), axis=(0, 1))
        s = s * log2e_scale + bias[t, :, lanes].reshape(2, 1, 8, 256)
        high = jnp.max(jnp.max(s, axis=(0, 1)), axis=0, keepdims=True)
        high = jnp.broadcast_to(jnp.maximum(high, FLOOR), (8, 256))
        mk[t, :, lanes] = high
        e = jnp.exp2(s - high)
        lk[t, :, lanes] = jnp.sum(e, axis=(0, 1))
        es[t, :, lanes] = e.reshape(256, 256)

    chunks = nq // 256
    for k in range(NZ):
        for slot in (2 * k, 2 * k + 1):
            if slot > 0:
                q_copy(BACK[slot]).wait_recv()
        if k > 0:
            p_copy(ZBACK[k]).wait_recv()
            f_copy(k).start()
        take_queries(2 * k)
        take_queries(2 * k + 1)
        f_copy(k).wait_recv()
        take_pair(k)
        set_bias(0, k + 1, slice(k * 256, (k + 1) * 256))
        if k > 0:
            set_bias(k, k + 1, slice(0, k * 256))
        for t in range(k):
            score_tile(t, k)
        for g in range(k + 1):
            score_tile(k, g)

    high = mk[0]
    for t in range(1, NZ):
        high = jnp.maximum(high, mk[t])
    total = jnp.zeros((8, nq), f32)
    for t in range(NZ):
        total += lk[t] * jnp.exp2(mk[t] - high)
    total = jnp.sum(total, axis=0, keepdims=True)
    st[...] = jnp.where(total > 0.0, high[0:1] + jnp.log2(jnp.where(total > 0.0, total, 1.0)), CLOSED)

    def n_copy(slot):
        return remote(st, nrm.at[BACK[slot]], n_ss.at[slot], n_rs.at[BACK[slot]], plane_peer(slot))

    for slot in range(PLANE - 1, 0, -1):
        n_copy(slot).start()
    parts = [st[...]]
    for slot in range(1, PLANE):
        n_copy(BACK[slot]).wait_recv()
        pieces = []
        for a, b in DXY:
            theirs = DXY.index(((a - DXY[slot][0]) % NX, (b - DXY[slot][1]) % NY))
            pieces.append(nrm[slot, :, theirs * rows:(theirs + 1) * rows])
        parts.append(jnp.concatenate(pieces, axis=1))
    high = parts[0]
    for part in parts[1:]:
        high = jnp.maximum(high, part)
    total = jnp.zeros((1, nq), f32)
    for part in parts:
        total += jnp.exp2(part - high)
    log_total = high + jnp.log2(total)
    for t in range(NZ):
        mk[t] = jnp.exp2(mk[t] - log_total)
    lsum = log_total[:, :rows] * math.log(2.0)

    def c_copy(t):
        return remote(cbuf.at[t], crecv.at[t], c_ss.at[t], c_rs.at[t], sibling)

    def z_copy(t):
        return remote(zsend.at[t], zrecv.at[ZBACK[t]], z_ss.at[t], z_rs.at[ZBACK[t]], z_peer(t))

    def y_copy(t):
        return remote(zstep.at[t], zstepr.at[ZBACK[t]], y_ss.at[t], y_rs.at[ZBACK[t]], z_peer(t))

    def combine(t):
        c_copy(t).wait_recv()
        both = own[t] + crecv[t]
        if t == 0:
            zown[...] = both
        else:
            zsend[t], zstep[t] = quantized(both)
            z_copy(t).start()
            y_copy(t).start()

    order = tuple(range(NZ - 1, -1, -1))
    for number, t in enumerate(order):
        for g in range(chunks):
            lanes = slice(g * 256, (g + 1) * 256)
            e = es[t, :, lanes].reshape(2, 16, 8, 256) * mk[t, :, lanes]
            target = tg[t, :, lanes].reshape(2, 1, 8, 256)
            w = jnp.where(within == target, e - 1.0, e).reshape(256, 256).astype(bf16)
            wts[t * 256:(t + 1) * 256, lanes] = w
        grad = jnp.zeros((256, width), f32)
        for g in range(chunks):
            grad += jnp.dot(
                wts[t * 256:(t + 1) * 256, g * 256:(g + 1) * 256],
                qall[2 * g:2 * g + 2, :rows, :].reshape(256, width),
                preferred_element_type=f32,
            )
        own[t] = grad[:rows]
        cbuf[t] = grad[rows:]
        c_copy(t).start()
        if number > 0:
            combine(order[number - 1])
    combine(order[-1])

    def g_copy(slot):
        return remote(qsend.at[slot], qrecv.at[BACK[slot]], g_ss.at[slot], g_rs.at[BACK[slot]], plane_peer(slot))

    def s_copy(slot):
        return remote(side.at[slot], sidr.at[BACK[slot]], s_ss.at[slot], s_rs.at[BACK[slot]], plane_peer(slot))

    eight = lax.broadcasted_iota(jnp.int32, (8, rows), 0)
    for g in range(chunks - 1, -1, -1):
        grad = jnp.dot(pt[...], wts[:, g * 256:(g + 1) * 256], preferred_element_type=f32)
        for half in range(2):
            slot = 2 * g + half
            piece = grad[:, half * rows:(half + 1) * rows]
            if slot == 0:
                qown[...] = piece
            else:
                qsend[slot], step = quantized(piece)
                found = jnp.sum(ps[:, slot * rows:(slot + 1) * rows], axis=0, keepdims=True)
                side[slot] = jnp.where(eight == 0, found, step)
                g_copy(slot).start()
                s_copy(slot).start()

    grads = zown[...]
    for t in range(1, NZ):
        z_copy(ZBACK[t]).wait_recv()
        y_copy(ZBACK[t]).wait_recv()
        grads += zrecv[t].astype(jnp.int32).astype(f32) * zstepr[t]
    pg_ref[...] = grads * scale

    found = jnp.sum(ps[:, :rows], axis=0, keepdims=True)
    grads = qown[...]
    for slot in range(PLANE - 1, 0, -1):
        g_copy(BACK[slot]).wait_recv()
        s_copy(BACK[slot]).wait_recv()
        found += sidr[slot, 0:1]
        grads += qrecv[slot].astype(jnp.int32).astype(f32) * sidr[slot, 1:2]
    loss_ref[...] = lsum - found * scale
    qg_ref[...] = (grads * scale).T

    for t in range(NZ):
        f_copy(t).wait_send()
        c_copy(t).wait_send()
    for t in range(1, NZ):
        p_copy(t).wait_send()
        z_copy(t).wait_send()
        y_copy(t).wait_send()
    for slot in range(1, PLANE):
        q_copy(slot).wait_send()
        n_copy(slot).wait_send()
        s_copy(slot).wait_send()
        g_copy(slot).wait_send()


def body(queries, pois, query_region, block_region, region_mask, positive):
    rows, width = queries.shape
    regions = region_mask.shape[0]
    nq = PLANE * rows
    npoi = 2 * NZ * rows
    vmem = pl.BlockSpec(memory_space=pltpu.VMEM)
    dma = pltpu.SemaphoreType.DMA
    loss, query_grad, poi_grad = pl.pallas_call(
        kernel,
        out_shape=(
            jax.ShapeDtypeStruct((1, rows), f32),
            jax.ShapeDtypeStruct((rows, width), f32),
            jax.ShapeDtypeStruct((rows, width), f32),
        ),
        in_specs=[vmem, vmem, vmem, vmem, pl.BlockSpec(memory_space=pltpu.SMEM), vmem],
        out_specs=(vmem, vmem, vmem),
        scratch_shapes=[
            pltpu.VMEM((PLANE, EXT, width), bf16),
            pltpu.VMEM((2 * NZ, EXT, width), bf16),
            pltpu.VMEM((width, npoi), bf16),
            pltpu.VMEM((regions, nq), bf16),
            pltpu.VMEM((16 * NZ, regions), bf16),
            pltpu.VMEM((NZ, 16, nq), f32),
            pltpu.VMEM((NZ, 16, nq), f32),
            pltpu.VMEM((NZ, 2 * rows, nq), f32),
            pltpu.VMEM((npoi, nq), bf16),
            pltpu.VMEM((NZ, 8, nq), f32),
            pltpu.VMEM((NZ, 8, nq), f32),
            pltpu.VMEM((8, nq), f32),
            pltpu.VMEM((1, nq), f32),
            pltpu.VMEM((PLANE, 1, nq), f32),
            pltpu.VMEM((PLANE, 8, rows), f32),
            pltpu.VMEM((PLANE, 8, rows), f32),
            pltpu.VMEM((NZ, rows, width), f32),
            pltpu.VMEM((NZ, rows, width), f32),
            pltpu.VMEM((NZ, rows, width), f32),
            pltpu.VMEM((rows, width), f32),
            pltpu.VMEM((NZ, rows, width), jnp.int16),
            pltpu.VMEM((NZ, rows, width), jnp.int16),
            pltpu.VMEM((NZ, 1, width), f32),
            pltpu.VMEM((NZ, 1, width), f32),
            pltpu.VMEM((width, rows), f32),
            pltpu.VMEM((PLANE, width, rows), jnp.int16),
            pltpu.VMEM((PLANE, width, rows), jnp.int16),
            dma((PLANE,)), dma((PLANE,)), dma((NZ,)), dma((NZ,)), dma((NZ,)), dma((NZ,)),
            dma((PLANE,)), dma((PLANE,)), dma((PLANE,)), dma((PLANE,)),
            dma((NZ,)), dma((NZ,)), dma((NZ,)), dma((NZ,)), dma((NZ,)), dma((NZ,)),
            dma((PLANE,)), dma((PLANE,)),
        ],
        compiler_params=pltpu.CompilerParams(
            collective_id=0, has_side_effects=True, vmem_limit_bytes=56 * 2**20
        ),
    )(
        queries, pois, query_region.reshape(1, rows), positive.reshape(1, rows), block_region, region_mask
    )
    return (loss.reshape(rows), query_grad, poi_grad)


def solution(mesh):
    in_specs = (
        P(("blk", "dp"), None),
        P(("blk", "dp"), None),
        P(("blk", "dp")),
        P(("blk", "dp")),
        P(),
        P(("blk", "dp")),
    )
    out_specs = (P(("blk", "dp")), P(("blk", "dp"), None), P(("blk", "dp"), None))
    return jax.shard_map(body, mesh=mesh, in_specs=in_specs, out_specs=out_specs, check_vma=False)
```

time: 116 us -> 71.6 us (0.62)
  Pallas kernels: 111 us -> 66.7 us
    pallas_call x1, Pallas kernels: 111 us -> 66.7 us  [body(): pl.pallas_call(kernel, out_shape=(jax.ShapeDtypeStruct((1, rows), f32), j...]
where the time goes in v2:
time: 71.6 us; the launch traced here: 71.5 us
  Pallas kernels  66.7 us (93%)
  local copies, waits for them, and re-layouts  3.44 us (5%)
  between operations  1.3 us (2%)
    pallas_call x1, Pallas kernels, body(): pl.pallas_call(kernel, out_shape=(jax.ShapeDtypeStruct((1, rows), f32), j...  66.7 us
    unnamed x7, local copies, waits for them, and re-layouts  3.44 us

profile of v2, /device:TPU:1, one launch (start us, length us, event | category | flops | bytes accessed | tf_op | source)
XLA Modules:
  0.0 71.5 jit_solution(7385696084090356110)
XLA Ops:
  1.3 66.7 %shard_map.85 = (f32[1,128]{1,0:T(1,128)}, f32[128,256]{1,0:T(8,128)}, f32[128,256]{1,0:T(8,128)}) custom-call(bf16[128,256]{1,0:T(8,128)(2,1)} %q_ref.1, bf16[128,256]{1,0:T(8,128)(2,1)} %p_ref.1, s32[1,128]{1,0:T(1,128)} %bitcast.3, s32[1,128]{1,0:T(1,128)} %bitcast.4, s32[1]{0:T(128)S(6)} %copy.12.breg_ref, s32[64,64]{1,0:T(8,128)} %mask_ref.1), custom_call_target="tpu_custom_call" | custom-call | tf_op jit(solution)/shard_map/pallas_call | solution.py:314
  68.0 0.0 copy-start.1
  68.0 0.7 copy-done.1
  68.7 0.5 copy.13
  69.2 0.0 copy-start
  69.2 1.6 %copy.14 = f32[128,256]{1,0:T(8,128)} copy(f32[128,256]{1,0:T(8,128)} %get-tuple-element.13) | data formatting | bytes 262144
  70.8 0.0 copy-done
  70.8 0.7 copy.15
Async XLA Ops:
  68.0 0.7 copy-start.1
  69.2 1.6 %copy-start = (f32[128,256]{1,0:T(8,128)S(1)}, f32[128,256]{1,0:T(8,128)}, u32[]{:S(2)}) copy-start(f32[128,256]{1,0:T(8,128)} %get-tuple-element.14) | copy-start | bytes 393220

commit v3 on v2

--- a/solution.py
+++ b/solution.py
@@ -9,16 +9,19 @@
 
 MESH = pl.DeviceIdType.MESH
 TILE = 128
-EXT = 144
+EXT = 136
 NX, NY, NZ = 4, 4, 8
 PLANE = NX * NY
 DZ = (0, 1, 7, 2, 6, 3, 5, 4)
 ZBACK = tuple(DZ.index((NZ - d) % NZ) for d in DZ)
 DXY = (
-    (0, 0), (1, 0), (3, 0), (0, 1), (0, 3), (1, 1), (3, 3), (1, 3),
-    (3, 1), (2, 0), (0, 2), (2, 1), (2, 3), (1, 2), (3, 2), (2, 2),
+    (0, 0), (1, 0), (3, 0), (0, 1), (0, 3), (2, 0), (0, 2), (1, 1),
+    (3, 3), (1, 3), (3, 1), (2, 1), (2, 3), (1, 2), (3, 2), (2, 2),
 )
 BACK = tuple(DXY.index(((NX - a) % NX, (NY - b) % NY)) for a, b in DXY)
+AXIS = 7
+HALF = 64
+LAG = 8
 CLOSED = -1e30
 FLOOR = -1e29
 TOP = 32767.0
@@ -38,7 +41,7 @@
     loss_ref, qg_ref, pg_ref,
     qall, pall, pt, hot, pick, tg, bias, es, wts, mk, lk, ps, st, nrm, side, sidr,
     own, cbuf, crecv, zown, zsend, zrecv, zstep, zstepr, qown, qsend, qrecv,
-    q_ss, q_rs, p_ss, p_rs, f_ss, f_rs, n_ss, n_rs, s_ss, s_rs,
+    q_ss, q_rs, h_ss, h_rs, p_ss, p_rs, f_ss, f_rs, n_ss, n_rs, s_ss, s_rs,
     c_ss, c_rs, z_ss, z_rs, y_ss, y_rs, g_ss, g_rs,
 ):
     blk = lax.axis_index("blk")
@@ -77,30 +80,59 @@
 
     qall[0, :rows, :] = q_ref[...]
     pall[0, :rows, :] = p_ref[...]
-    row = lax.broadcasted_iota(jnp.int32, (16, rows), 0)
+    row = lax.broadcasted_iota(jnp.int32, (EXT - rows, rows), 0)
     pos = pos_ref[...]
     small = jnp.where(row == 0, reg_ref[...], jnp.where(row == 1, pos // TILE, pos % TILE)).astype(f32)
     small = small.astype(bf16)
     qall[0, rows:, :rows] = small
     qall[0, rows:, rows:] = small
-    pall[0, rows:, :] = jnp.full((16, width), breg_ref[0], jnp.int32).astype(f32).astype(bf16)
+    pall[0, rows:, :] = jnp.full((EXT - rows, width), breg_ref[0], jnp.int32).astype(f32).astype(bf16)
 
     pl.semaphore_wait(barrier, PLANE + NZ - 1)
 
     def q_copy(slot):
         return remote(qall.at[0], qall.at[BACK[slot]], q_ss.at[slot], q_rs.at[BACK[slot]], plane_peer(slot))
 
-    def p_copy(t):
-        return remote(pall.at[0], pall.at[2 * ZBACK[t]], p_ss.at[t], p_rs.at[ZBACK[t]], z_peer(t))
+    def h_copy(slot, peer):
+        a, b = DXY[slot]
+        c, d = DXY[peer]
+        there = DXY.index(((a - c) % NX, (b - d) % NY))
+        part = slice(0, HALF) if b == 0 else slice(HALF, EXT)
+        k = 2 * there + (0 if b == 0 else 1)
+        return remote(qall.at[slot, part], qall.at[there, part], h_ss.at[k], h_rs.at[k], plane_peer(peer))
+
+    def pass_on(slot):
+        a, b = DXY[slot]
+        return [h_copy(slot, DXY.index((0, d) if b == 0 else (d, 0))) for d in (1, 3, 2)]
+
+    def p_copy(slot, part, t, k, dz):
+        return remote(pall.at[2 * slot, part], pall.at[2 * t, part], p_ss.at[k], p_rs.at[k], z_peer(DZ.index(dz)))
+
+    def p_next(t):
+        whole, low, high = slice(0, EXT), slice(0, HALF), slice(HALF, EXT)
+        if t == 0:
+            return [p_copy(0, whole, ZBACK[k], ZBACK[k], DZ[k]) for k in (3, 4, 1, 2)]
+        if DZ[t] == 2:
+            return [p_copy(t, low, 7, 7, NZ - 2), p_copy(t, whole, 5, 5, NZ - 1)]
+        if DZ[t] == 6:
+            return [p_copy(t, high, 7, 8, 2), p_copy(t, whole, 6, 6, 1)]
+        return []
+
+    def p_wait(t):
+        if t < 7:
+            p_copy(0, slice(0, EXT), t, t, 1).wait_recv()
+        else:
+            p_copy(0, slice(0, HALF), 7, 7, 1).wait_recv()
+            p_copy(0, slice(HALF, EXT), 7, 8, 1).wait_recv()
 
     def f_copy(t):
         return remote(pall.at[2 * t], pall.at[2 * t + 1], f_ss.at[t], f_rs.at[t], sibling)
 
+    for copy in p_next(0):
+        copy.start()
+    for slot in range(1, AXIS):
+        q_copy(slot).start()
     f_copy(0).start()
-    for slot in range(1, PLANE):
-        q_copy(slot).start()
-        if slot < NZ:
-            p_copy(slot).start()
 
     ps[...] = jnp.zeros_like(ps)
     region_mask = mask_ref[...].astype(f32).astype(bf16)
@@ -159,24 +191,53 @@
         es[t, :, lanes] = e.reshape(256, 256)
 
     chunks = nq // 256
-    for k in range(NZ):
-        for slot in (2 * k, 2 * k + 1):
-            if slot > 0:
-                q_copy(BACK[slot]).wait_recv()
-        if k > 0:
-            p_copy(ZBACK[k]).wait_recv()
-            f_copy(k).start()
-        take_queries(2 * k)
-        take_queries(2 * k + 1)
-        f_copy(k).wait_recv()
-        take_pair(k)
-        set_bias(0, k + 1, slice(k * 256, (k + 1) * 256))
-        if k > 0:
-            set_bias(k, k + 1, slice(0, k * 256))
-        for t in range(k):
-            score_tile(t, k)
-        for g in range(k + 1):
-            score_tile(k, g)
+    ready = {"t": 0, "g": 0}
+
+    def arrived_queries(slot):
+        if slot > 0:
+            q_copy(BACK[slot]).wait_recv()
+            for copy in pass_on(slot):
+                copy.start()
+        take_queries(slot)
+
+    def arrived_shard(t):
+        p_wait(t)
+        for copy in p_next(t):
+            copy.start()
+        f_copy(t).start()
+
+    def use_pair(t):
+        f_copy(t).wait_recv()
+        take_pair(t)
+        ready["t"] = t + 1
+        if ready["g"]:
+            set_bias(t, t + 1, slice(0, ready["g"] * 256))
+        for g in range(ready["g"]):
+            score_tile(t, g)
+
+    def use_chunk(g):
+        for slot in (2 * g, 2 * g + 1):
+            if slot >= AXIS:
+                for half in range(2):
+                    part = slice(0, HALF) if half == 0 else slice(HALF, EXT)
+                    k = 2 * slot + half
+                    remote(qall.at[slot, part], qall.at[slot, part], h_ss.at[k], h_rs.at[k], sibling).wait_recv()
+                take_queries(slot)
+        ready["g"] = g + 1
+        if ready["t"]:
+            set_bias(0, ready["t"], slice(g * 256, (g + 1) * 256))
+        for t in range(ready["t"]):
+            score_tile(t, g)
+
+    steps = (
+        (arrived_queries, (0, 1, 2, 3, 4)), (arrived_shard, (3, 4)), (arrived_queries, (5, 6)), (arrived_shard, (1, 2)),
+        (use_pair, (0,)), (use_chunk, (0, 1, 2)), (use_pair, (1, 2, 3, 4)), (use_chunk, (3, 4)),
+        (arrived_shard, (5, 6)), (use_chunk, (5,)), (arrived_shard, (7,)), (use_pair, (5, 6)), (use_chunk, (6, 7)),
+        (use_pair, (7,)),
+    )
+    for step, items in steps:
+        for item in items:
+            step(item)
 
     high = mk[0]
     for t in range(1, NZ):
@@ -248,9 +309,9 @@
         own[t] = grad[:rows]
         cbuf[t] = grad[rows:]
         c_copy(t).start()
-        if number > 0:
-            combine(order[number - 1])
-    combine(order[-1])
+        if number >= LAG:
+            combine(order[number - LAG])
+    late = list(order[NZ - LAG:])
 
     def g_copy(slot):
         return remote(qsend.at[slot], qrecv.at[BACK[slot]], g_ss.at[slot], g_rs.at[BACK[slot]], plane_peer(slot))
@@ -272,6 +333,7 @@
                 side[slot] = jnp.where(eight == 0, found, step)
                 g_copy(slot).start()
                 s_copy(slot).start()
+        combine(late.pop(0))
 
     grads = zown[...]
     for t in range(1, NZ):
@@ -293,15 +355,19 @@
     for t in range(NZ):
         f_copy(t).wait_send()
         c_copy(t).wait_send()
+        for copy in p_next(t):
+            copy.wait_send()
     for t in range(1, NZ):
-        p_copy(t).wait_send()
         z_copy(t).wait_send()
         y_copy(t).wait_send()
     for slot in range(1, PLANE):
-        q_copy(slot).wait_send()
         n_copy(slot).wait_send()
         s_copy(slot).wait_send()
         g_copy(slot).wait_send()
+    for slot in range(1, AXIS):
+        q_copy(slot).wait_send()
+        for copy in pass_on(slot):
+            copy.wait_send()
 
 
 def body(queries, pois, query_region, block_region, region_mask, positive):
@@ -348,8 +414,8 @@
             pltpu.VMEM((width, rows), f32),
             pltpu.VMEM((PLANE, width, rows), jnp.int16),
             pltpu.VMEM((PLANE, width, rows), jnp.int16),
-            dma((PLANE,)), dma((PLANE,)), dma((NZ,)), dma((NZ,)), dma((NZ,)), dma((NZ,)),
-            dma((PLANE,)), dma((PLANE,)), dma((PLANE,)), dma((PLANE,)),
+            dma((PLANE,)), dma((PLANE,)), dma((2 * PLANE,)), dma((2 * PLANE,)), dma((NZ + 1,)), dma((NZ + 1,)),
+            dma((NZ,)), dma((NZ,)), dma((PLANE,)), dma((PLANE,)), dma((PLANE,)), dma((PLANE,)),
             dma((NZ,)), dma((NZ,)), dma((NZ,)), dma((NZ,)), dma((NZ,)), dma((NZ,)),
             dma((PLANE,)), dma((PLANE,)),
         ],

time: 71.6 us -> 62.7 us (0.88)
  Pallas kernels: 66.7 us -> 57.8 us
    pallas_call x1, Pallas kernels: 66.7 us -> 57.8 us  [body(): pl.pallas_call(kernel, out_shape=(jax.ShapeDtypeStruct((1, rows), f32), j...]
where the time goes in v3:
time: 62.7 us; the launch traced here: 62.6 us
  Pallas kernels  57.8 us (92%)
  local copies, waits for them, and re-layouts  3.44 us (5%)
  between operations  1.3 us (2%)
    pallas_call x1, Pallas kernels, body(): pl.pallas_call(kernel, out_shape=(jax.ShapeDtypeStruct((1, rows), f32), j...  57.8 us
    unnamed x7, local copies, waits for them, and re-layouts  3.44 us

profile of v3, /device:TPU:1, one launch (start us, length us, event | category | flops | bytes accessed | tf_op | source)
XLA Modules:
  0.0 62.6 jit_solution(5810955830248717444)
XLA Ops:
  1.3 57.8 %shard_map.85 = (f32[1,128]{1,0:T(1,128)}, f32[128,256]{1,0:T(8,128)}, f32[128,256]{1,0:T(8,128)}) custom-call(bf16[128,256]{1,0:T(8,128)(2,1)} %q_ref.1, bf16[128,256]{1,0:T(8,128)(2,1)} %p_ref.1, s32[1,128]{1,0:T(1,128)} %bitcast.3, s32[1,128]{1,0:T(1,128)} %bitcast.4, s32[1]{0:T(128)S(6)} %copy.12.breg_ref, s32[64,64]{1,0:T(8,128)} %mask_ref.1), custom_call_target="tpu_custom_call" | custom-call | tf_op jit(solution)/shard_map/pallas_call | solution.py:380
  59.1 0.0 copy-start.1
  59.1 0.7 %copy-done.1 = f32[1,128]{1,0:T(1,128)S(1)} copy-done((f32[1,128]{1,0:T(1,128)S(1)}, f32[1,128]{1,0:T(1,128)}, u32[]{:S(2)}) %copy-start.1) | copy-done | bytes 536
  59.8 0.5 copy.13
  60.3 0.0 copy-start
  60.3 1.6 %copy.14 = f32[128,256]{1,0:T(8,128)} copy(f32[128,256]{1,0:T(8,128)} %get-tuple-element.13) | data formatting | bytes 262144
  61.9 0.0 copy-done
  61.9 0.7 %copy.15 = f32[128,256]{1,0:T(8,128)} copy(f32[128,256]{1,0:T(8,128)S(1)} %copy-done) | data formatting | bytes 262144
Async XLA Ops:
  59.1 0.7 %copy-start.1 = (f32[1,128]{1,0:T(1,128)S(1)}, f32[1,128]{1,0:T(1,128)}, u32[]{:S(2)}) copy-start(f32[1,128]{1,0:T(1,128)} %get-tuple-element.6) | copy-start | bytes 1540
  60.3 1.6 %copy-start = (f32[128,256]{1,0:T(8,128)S(1)}, f32[128,256]{1,0:T(8,128)}, u32[]{:S(2)}) copy-start(f32[128,256]{1,0:T(8,128)} %get-tuple-element.14) | copy-start | bytes 393220

commit v4 on v3

--- a/solution.py
+++ b/solution.py
@@ -21,7 +21,7 @@
 BACK = tuple(DXY.index(((NX - a) % NX, (NY - b) % NY)) for a, b in DXY)
 AXIS = 7
 HALF = 64
-LAG = 8
+LAG = 2
 CLOSED = -1e30
 FLOOR = -1e29
 TOP = 32767.0
@@ -40,7 +40,7 @@
     q_ref, p_ref, reg_ref, pos_ref, breg_ref, mask_ref,
     loss_ref, qg_ref, pg_ref,
     qall, pall, pt, hot, pick, tg, bias, es, wts, mk, lk, ps, st, nrm, side, sidr,
-    own, cbuf, crecv, zown, zsend, zrecv, zstep, zstepr, qown, qsend, qrecv,
+    own, cbuf, crecv, zsend, zrecv, relay, relay_half, zstep, zstepr, qown, qsend, qrecv,
     q_ss, q_rs, h_ss, h_rs, p_ss, p_rs, f_ss, f_rs, n_ss, n_rs, s_ss, s_rs,
     c_ss, c_rs, z_ss, z_rs, y_ss, y_rs, g_ss, g_rs,
 ):
@@ -272,33 +272,76 @@
         mk[t] = jnp.exp2(mk[t] - log_total)
     lsum = log_total[:, :rows] * math.log(2.0)
 
-    def c_copy(t):
-        return remote(cbuf.at[t], crecv.at[t], c_ss.at[t], c_rs.at[t], sibling)
-
-    def z_copy(t):
-        return remote(zsend.at[t], zrecv.at[ZBACK[t]], z_ss.at[t], z_rs.at[ZBACK[t]], z_peer(t))
-
-    def y_copy(t):
-        return remote(zstep.at[t], zstepr.at[ZBACK[t]], y_ss.at[t], y_rs.at[ZBACK[t]], z_peer(t))
-
-    def combine(t):
-        c_copy(t).wait_recv()
-        both = own[t] + crecv[t]
-        if t == 0:
-            zown[...] = both
-        else:
-            zsend[t], zstep[t] = quantized(both)
-            z_copy(t).start()
-            y_copy(t).start()
-
-    order = tuple(range(NZ - 1, -1, -1))
-    for number, t in enumerate(order):
-        for g in range(chunks):
-            lanes = slice(g * 256, (g + 1) * 256)
+    def g_copy(slot):
+        return remote(qsend.at[slot], qrecv.at[BACK[slot]], g_ss.at[slot], g_rs.at[BACK[slot]], plane_peer(slot))
+
+    def s_copy(slot):
+        return remote(side.at[slot], sidr.at[BACK[slot]], s_ss.at[slot], s_rs.at[BACK[slot]], plane_peer(slot))
+
+    eight = lax.broadcasted_iota(jnp.int32, (8, rows), 0)
+    for g in range(chunks - 1, -1, -1):
+        lanes = slice(g * 256, (g + 1) * 256)
+        for t in range(NZ):
             e = es[t, :, lanes].reshape(2, 16, 8, 256) * mk[t, :, lanes]
             target = tg[t, :, lanes].reshape(2, 1, 8, 256)
             w = jnp.where(within == target, e - 1.0, e).reshape(256, 256).astype(bf16)
             wts[t * 256:(t + 1) * 256, lanes] = w
+        grad = jnp.dot(pt[...], wts[:, g * 256:(g + 1) * 256], preferred_element_type=f32)
+        for half in range(2):
+            slot = 2 * g + half
+            piece = grad[:, half * rows:(half + 1) * rows]
+            if slot == 0:
+                qown[...] = piece
+            else:
+                qsend[slot], step = quantized(piece)
+                found = jnp.sum(ps[:, slot * rows:(slot + 1) * rows], axis=0, keepdims=True)
+                side[slot] = jnp.where(eight == 0, found, step)
+                g_copy(slot).start()
+                s_copy(slot).start()
+
+    def c_copy(t):
+        return remote(cbuf.at[t], crecv.at[t], c_ss.at[t], c_rs.at[t], sibling)
+
+    low, high = slice(0, HALF), slice(HALF, rows)
+    moves = {
+        5: (zsend.at[5], relay.at[0], 1, 5), 6: (zsend.at[6], relay.at[1], 2, 6),
+        7: (zsend.at[7, low], relay_half.at[0], 3, 7), 8: (zsend.at[7, high], relay_half.at[1], 4, 8),
+        1: (zsend.at[1], zrecv.at[2], 1, 2), 2: (zsend.at[2], zrecv.at[1], 2, 1),
+        3: (zsend.at[3], zrecv.at[4], 3, 4), 4: (zsend.at[4], zrecv.at[3], 4, 3),
+    }
+
+    def z_copies(k):
+        src, dst, peer, there = moves[k]
+        return (
+            remote(src, dst, z_ss.at[k], z_rs.at[there], z_peer(peer)),
+            remote(zstep.at[k], zstepr.at[there], y_ss.at[k], y_rs.at[there], z_peer(peer)),
+        )
+
+    def z_send(k):
+        for copy in z_copies(k):
+            copy.start()
+
+    def z_arrived(there):
+        for k in moves:
+            if moves[k][3] == there:
+                for copy in z_copies(k):
+                    copy.wait_recv()
+
+    def combine(t):
+        c_copy(t).wait_recv()
+        both = own[t] + crecv[t]
+        if t in (0, 3, 4):
+            own[t] = both
+        elif t == 7:
+            for k, part in ((7, low), (8, high)):
+                zsend[t, part], zstep[k] = quantized(both[part])
+                z_send(k)
+        else:
+            zsend[t], zstep[t] = quantized(both)
+            z_send(t)
+
+    order = (5, 6, 7, 1, 2, 3, 4, 0)
+    for number, t in enumerate(order):
         grad = jnp.zeros((256, width), f32)
         for g in range(chunks):
             grad += jnp.dot(
@@ -311,36 +354,21 @@
         c_copy(t).start()
         if number >= LAG:
             combine(order[number - LAG])
-    late = list(order[NZ - LAG:])
-
-    def g_copy(slot):
-        return remote(qsend.at[slot], qrecv.at[BACK[slot]], g_ss.at[slot], g_rs.at[BACK[slot]], plane_peer(slot))
-
-    def s_copy(slot):
-        return remote(side.at[slot], sidr.at[BACK[slot]], s_ss.at[slot], s_rs.at[BACK[slot]], plane_peer(slot))
-
-    eight = lax.broadcasted_iota(jnp.int32, (8, rows), 0)
-    for g in range(chunks - 1, -1, -1):
-        grad = jnp.dot(pt[...], wts[:, g * 256:(g + 1) * 256], preferred_element_type=f32)
-        for half in range(2):
-            slot = 2 * g + half
-            piece = grad[:, half * rows:(half + 1) * rows]
-            if slot == 0:
-                qown[...] = piece
-            else:
-                qsend[slot], step = quantized(piece)
-                found = jnp.sum(ps[:, slot * rows:(slot + 1) * rows], axis=0, keepdims=True)
-                side[slot] = jnp.where(eight == 0, found, step)
-                g_copy(slot).start()
-                s_copy(slot).start()
-        combine(late.pop(0))
-
-    grads = zown[...]
-    for t in range(1, NZ):
-        z_copy(ZBACK[t]).wait_recv()
-        y_copy(ZBACK[t]).wait_recv()
-        grads += zrecv[t].astype(jnp.int32).astype(f32) * zstepr[t]
-    pg_ref[...] = grads * scale
+    for t in order[NZ - LAG:]:
+        combine(t)
+
+    def decoded(v, step):
+        return v.astype(jnp.int32).astype(f32) * step
+
+    for side_no, t in enumerate((3, 4)):
+        z_arrived(5 + side_no)
+        z_arrived(7 + side_no)
+        both = own[t] + decoded(relay[side_no], zstepr[5 + side_no])
+        half = decoded(relay_half[side_no], zstepr[7 + side_no])
+        halves = [both[:HALF], both[HALF:]]
+        halves[side_no] += half
+        zsend[t], zstep[t] = quantized(jnp.concatenate(halves, axis=0))
+        z_send(t)
 
     found = jnp.sum(ps[:, :rows], axis=0, keepdims=True)
     grads = qown[...]
@@ -348,18 +376,24 @@
         g_copy(BACK[slot]).wait_recv()
         s_copy(BACK[slot]).wait_recv()
         found += sidr[slot, 0:1]
-        grads += qrecv[slot].astype(jnp.int32).astype(f32) * sidr[slot, 1:2]
+        grads += decoded(qrecv[slot], sidr[slot, 1:2])
     loss_ref[...] = lsum - found * scale
-    qg_ref[...] = (grads * scale).T
+    qg_ref[...] = grads
+
+    grads = own[0]
+    for t in range(1, 5):
+        z_arrived(t)
+        grads += decoded(zrecv[t], zstepr[t])
+    pg_ref[...] = grads
 
     for t in range(NZ):
         f_copy(t).wait_send()
         c_copy(t).wait_send()
         for copy in p_next(t):
             copy.wait_send()
-    for t in range(1, NZ):
-        z_copy(t).wait_send()
-        y_copy(t).wait_send()
+    for k in moves:
+        for copy in z_copies(k):
+            copy.wait_send()
     for slot in range(1, PLANE):
         n_copy(slot).wait_send()
         s_copy(slot).wait_send()
@@ -368,6 +402,13 @@
         q_copy(slot).wait_send()
         for copy in pass_on(slot):
             copy.wait_send()
+
+
+def finish(loss_ref, qt_ref, pg_ref, loss_out, qg_out, pg_out):
+    scale = 1.0 / math.sqrt(pg_ref.shape[1])
+    loss_out[...] = loss_ref[...]
+    qg_out[...] = (qt_ref[...] * scale).T
+    pg_out[...] = pg_ref[...] * scale
 
 
 def body(queries, pois, query_region, block_region, region_mask, positive):
@@ -381,7 +422,7 @@
         kernel,
         out_shape=(
             jax.ShapeDtypeStruct((1, rows), f32),
-            jax.ShapeDtypeStruct((rows, width), f32),
+            jax.ShapeDtypeStruct((width, rows), f32),
             jax.ShapeDtypeStruct((rows, width), f32),
         ),
         in_specs=[vmem, vmem, vmem, vmem, pl.BlockSpec(memory_space=pltpu.SMEM), vmem],
@@ -406,17 +447,18 @@
             pltpu.VMEM((NZ, rows, width), f32),
             pltpu.VMEM((NZ, rows, width), f32),
             pltpu.VMEM((NZ, rows, width), f32),
-            pltpu.VMEM((rows, width), f32),
             pltpu.VMEM((NZ, rows, width), jnp.int16),
-            pltpu.VMEM((NZ, rows, width), jnp.int16),
-            pltpu.VMEM((NZ, 1, width), f32),
-            pltpu.VMEM((NZ, 1, width), f32),
+            pltpu.VMEM((5, rows, width), jnp.int16),
+            pltpu.VMEM((2, rows, width), jnp.int16),
+            pltpu.VMEM((2, HALF, width), jnp.int16),
+            pltpu.VMEM((NZ + 1, 1, width), f32),
+            pltpu.VMEM((NZ + 1, 1, width), f32),
             pltpu.VMEM((width, rows), f32),
             pltpu.VMEM((PLANE, width, rows), jnp.int16),
             pltpu.VMEM((PLANE, width, rows), jnp.int16),
             dma((PLANE,)), dma((PLANE,)), dma((2 * PLANE,)), dma((2 * PLANE,)), dma((NZ + 1,)), dma((NZ + 1,)),
             dma((NZ,)), dma((NZ,)), dma((PLANE,)), dma((PLANE,)), dma((PLANE,)), dma((PLANE,)),
-            dma((NZ,)), dma((NZ,)), dma((NZ,)), dma((NZ,)), dma((NZ,)), dma((NZ,)),
+            dma((NZ,)), dma((NZ,)), dma((NZ + 1,)), dma((NZ + 1,)), dma((NZ + 1,)), dma((NZ + 1,)),
             dma((PLANE,)), dma((PLANE,)),
         ],
         compiler_params=pltpu.CompilerParams(
@@ -425,6 +467,16 @@
     )(
         queries, pois, query_region.reshape(1, rows), positive.reshape(1, rows), block_region, region_mask
     )
+    loss, query_grad, poi_grad = pl.pallas_call(
+        finish,
+        out_shape=(
+            jax.ShapeDtypeStruct((1, rows), f32),
+            jax.ShapeDtypeStruct((rows, width), f32),
+            jax.ShapeDtypeStruct((rows, width), f32),
+        ),
+        in_specs=[vmem, vmem, vmem],
+        out_specs=(vmem, vmem, vmem),
+    )(loss, query_grad, poi_grad)
     return (loss.reshape(rows), query_grad, poi_grad)
 
 

time: 62.7 us -> 56.2 us (0.90)
  local copies, waits for them, and re-layouts: 3.44 us -> 0 us
  Pallas kernels: 57.8 us -> 54.7 us
    pallas_call x1, Pallas kernels: 57.8 us -> 53 us  [body(): pl.pallas_call(kernel, out_shape=(jax.ShapeDtypeStruct((1, rows), f32), j...]
    unnamed x7 -> x0, local copies, waits for them, and re-layouts: 3.44 us -> none
    pallas_call x0 -> x1, Pallas kernels: none -> 1.77 us  [body(): pl.pallas_call(finish, out_shape=(jax.ShapeDtypeStruct((1, rows), f32), j...]
where the time goes in v4:
time: 56.2 us; the launch traced here: 56 us
  Pallas kernels  54.7 us (97%)
  between operations  1.29 us (2%)
    pallas_call x1, Pallas kernels, body(): pl.pallas_call(kernel, out_shape=(jax.ShapeDtypeStruct((1, rows), f32), j...  53 us
    pallas_call x1, Pallas kernels, body(): pl.pallas_call(finish, out_shape=(jax.ShapeDtypeStruct((1, rows), f32), j...  1.77 us

profile of v4, /device:TPU:1, one launch (start us, length us, event | category | flops | bytes accessed | tf_op | source)
XLA Modules:
  0.0 56.0 jit_solution(7281448305473096741)
XLA Ops:
  1.3 53.0 %shard_map.85 = (f32[1,128]{1,0:T(1,128)}, f32[256,128]{1,0:T(8,128)}, f32[128,256]{1,0:T(8,128)}) custom-call(bf16[128,256]{1,0:T(8,128)(2,1)} %q_ref.1, bf16[128,256]{1,0:T(8,128)(2,1)} %p_ref.1, s32[1,128]{1,0:T(1,128)} %bitcast.3, s32[1,128]{1,0:T(1,128)} %bitcast.4, s32[1]{0:T(128)S(6)} %copy.9.breg_ref, s32[64,64]{1,0:T(8,128)} %mask_ref.1), custom_call_target="tpu_custom_call" | custom-call | tf_op jit(solution)/shard_map/pallas_call | solution.py:421
  54.2 1.8 %shard_map.86 = (f32[1,128]{1,0:T(1,128)}, f32[128,256]{1,0:T(8,128)}, f32[128,256]{1,0:T(8,128)}) custom-call(f32[1,128]{1,0:T(1,128)} %get-tuple-element.9.loss_ref, f32[256,128]{1,0:T(8,128)} %get-tuple-element.10.qt_ref, f32[128,256]{1,0:T(8,128)} %get-tuple-element.11.pg_ref), custom_call_target="tpu_custom_call" | custom-call | tf_op jit(solution)/shard_map/pallas_call | solution.py:470

commit v5 on v4

--- a/solution.py
+++ b/solution.py
@@ -39,10 +39,10 @@
 def kernel(
     q_ref, p_ref, reg_ref, pos_ref, breg_ref, mask_ref,
     loss_ref, qg_ref, pg_ref,
-    qall, pall, pt, hot, pick, tg, bias, es, wts, mk, lk, ps, st, nrm, side, sidr,
-    own, cbuf, crecv, zsend, zrecv, relay, relay_half, zstep, zstepr, qown, qsend, qrecv,
+    regs, poss, masks, l_ss, qall, pall, pt, hot, pick, tg, bias, es, wts, mk, lk, ps, st, nrm, side, sidr,
+    own, cbuf, crecv, zsend, zrecv, relay, relay_half, zstep, zstepr, qown, gsend, grecv, gstep, gstepr, esend, erecv, estep, estepr,
     q_ss, q_rs, h_ss, h_rs, p_ss, p_rs, f_ss, f_rs, n_ss, n_rs, s_ss, s_rs,
-    c_ss, c_rs, z_ss, z_rs, y_ss, y_rs, g_ss, g_rs,
+    c_ss, c_rs, z_ss, z_rs, y_ss, y_rs, g_ss, g_rs, i_ss, i_rs, e_ss, e_rs, j_ss, j_rs,
 ):
     blk = lax.axis_index("blk")
     dp = lax.axis_index("dp")
@@ -71,24 +71,31 @@
             src_ref=src, dst_ref=dst, send_sem=ss, recv_sem=rs, device_id=dev, device_id_type=MESH
         )
 
+    loads = [
+        pltpu.make_async_copy(src, dst, l_ss.at[k])
+        for k, (src, dst) in enumerate((
+            (reg_ref, regs), (pos_ref, poss), (mask_ref, masks),
+            (q_ref, qall.at[0, :rows, :]), (p_ref, pall.at[0, :rows, :]),
+        ))
+    ]
+    for load in loads:
+        load.start()
     barrier = pltpu.get_barrier_semaphore()
-    for slot in range(1, PLANE):
-        pl.semaphore_signal(barrier, inc=1, device_id=plane_peer(slot), device_id_type=MESH)
-    for t in range(1, NZ):
-        pl.semaphore_signal(barrier, inc=1, device_id=z_peer(t), device_id_type=MESH)
-    pl.semaphore_signal(barrier, inc=1, device_id=sibling, device_id_type=MESH)
-
-    qall[0, :rows, :] = q_ref[...]
-    pall[0, :rows, :] = p_ref[...]
+    near = [plane_peer(slot) for slot in range(1, PLANE)] + [z_peer(t) for t in range(1, 5)] + [sibling]
+    for peer in near:
+        pl.semaphore_signal(barrier, inc=1, device_id=peer, device_id_type=MESH)
+
+    for load in loads:
+        load.wait()
     row = lax.broadcasted_iota(jnp.int32, (EXT - rows, rows), 0)
-    pos = pos_ref[...]
-    small = jnp.where(row == 0, reg_ref[...], jnp.where(row == 1, pos // TILE, pos % TILE)).astype(f32)
+    pos = poss[...]
+    small = jnp.where(row == 0, regs[...], jnp.where(row == 1, pos // TILE, pos % TILE)).astype(f32)
     small = small.astype(bf16)
     qall[0, rows:, :rows] = small
     qall[0, rows:, rows:] = small
     pall[0, rows:, :] = jnp.full((EXT - rows, width), breg_ref[0], jnp.int32).astype(f32).astype(bf16)
 
-    pl.semaphore_wait(barrier, PLANE + NZ - 1)
+    pl.semaphore_wait(barrier, len(near))
 
     def q_copy(slot):
         return remote(qall.at[0], qall.at[BACK[slot]], q_ss.at[slot], q_rs.at[BACK[slot]], plane_peer(slot))
@@ -135,7 +142,7 @@
     f_copy(0).start()
 
     ps[...] = jnp.zeros_like(ps)
-    region_mask = mask_ref[...].astype(f32).astype(bf16)
+    region_mask = masks[...].astype(f32).astype(bf16)
     regions = region_mask.shape[0]
     region_ids = lax.broadcasted_iota(jnp.int32, (regions, rows), 0).astype(f32)
     lane_ids = lax.broadcasted_iota(jnp.int32, (8, regions), 1).astype(f32)
@@ -251,8 +258,14 @@
     def n_copy(slot):
         return remote(st, nrm.at[BACK[slot]], n_ss.at[slot], n_rs.at[BACK[slot]], plane_peer(slot))
 
+    def s_copy(slot):
+        return remote(side.at[slot], sidr.at[BACK[slot]], s_ss.at[slot], s_rs.at[BACK[slot]], plane_peer(slot))
+
     for slot in range(PLANE - 1, 0, -1):
         n_copy(slot).start()
+    for slot in range(PLANE - 1, 0, -1):
+        side[slot] = jnp.sum(ps[:, slot * rows:(slot + 1) * rows], axis=0, keepdims=True)
+        s_copy(slot).start()
     parts = [st[...]]
     for slot in range(1, PLANE):
         n_copy(BACK[slot]).wait_recv()
@@ -272,33 +285,6 @@
         mk[t] = jnp.exp2(mk[t] - log_total)
     lsum = log_total[:, :rows] * math.log(2.0)
 
-    def g_copy(slot):
-        return remote(qsend.at[slot], qrecv.at[BACK[slot]], g_ss.at[slot], g_rs.at[BACK[slot]], plane_peer(slot))
-
-    def s_copy(slot):
-        return remote(side.at[slot], sidr.at[BACK[slot]], s_ss.at[slot], s_rs.at[BACK[slot]], plane_peer(slot))
-
-    eight = lax.broadcasted_iota(jnp.int32, (8, rows), 0)
-    for g in range(chunks - 1, -1, -1):
-        lanes = slice(g * 256, (g + 1) * 256)
-        for t in range(NZ):
-            e = es[t, :, lanes].reshape(2, 16, 8, 256) * mk[t, :, lanes]
-            target = tg[t, :, lanes].reshape(2, 1, 8, 256)
-            w = jnp.where(within == target, e - 1.0, e).reshape(256, 256).astype(bf16)
-            wts[t * 256:(t + 1) * 256, lanes] = w
-        grad = jnp.dot(pt[...], wts[:, g * 256:(g + 1) * 256], preferred_element_type=f32)
-        for half in range(2):
-            slot = 2 * g + half
-            piece = grad[:, half * rows:(half + 1) * rows]
-            if slot == 0:
-                qown[...] = piece
-            else:
-                qsend[slot], step = quantized(piece)
-                found = jnp.sum(ps[:, slot * rows:(slot + 1) * rows], axis=0, keepdims=True)
-                side[slot] = jnp.where(eight == 0, found, step)
-                g_copy(slot).start()
-                s_copy(slot).start()
-
     def c_copy(t):
         return remote(cbuf.at[t], crecv.at[t], c_ss.at[t], c_rs.at[t], sibling)
 
@@ -340,8 +326,33 @@
             zsend[t], zstep[t] = quantized(both)
             z_send(t)
 
-    order = (5, 6, 7, 1, 2, 3, 4, 0)
-    for number, t in enumerate(order):
+    def line(way, d):
+        return DXY.index((d, 0) if way == 0 else (0, d))
+
+    def g_copies(way, d, e):
+        k, there = 16 * way + 4 * d + e, 16 * way + 4 * ((4 - d) % 4) + e
+        peer = plane_peer(line(way, d))
+        return (
+            remote(gsend.at[k], grecv.at[there], g_ss.at[k], g_rs.at[there], peer),
+            remote(gstep.at[k], gstepr.at[there], i_ss.at[k], i_rs.at[there], peer),
+        )
+
+    def e_copies(way, d):
+        k, there = 4 * way + d, 4 * way + (4 - d) % 4
+        peer = plane_peer(line(1 - way, d))
+        return (
+            remote(esend.at[k], erecv.at[there], e_ss.at[k], e_rs.at[there], peer),
+            remote(estep.at[k], estepr.at[there], j_ss.at[k], j_rs.at[there], peer),
+        )
+
+    def set_weights(t, g):
+        lanes = slice(g * 256, (g + 1) * 256)
+        e = es[t, :, lanes].reshape(2, 16, 8, 256) * mk[t, :, lanes]
+        target = tg[t, :, lanes].reshape(2, 1, 8, 256)
+        w = jnp.where(within == target, e - 1.0, e).reshape(256, 256).astype(bf16)
+        wts[t * 256:(t + 1) * 256, lanes] = w
+
+    def poi_step(t):
         grad = jnp.zeros((256, width), f32)
         for g in range(chunks):
             grad += jnp.dot(
@@ -352,14 +363,64 @@
         own[t] = grad[:rows]
         cbuf[t] = grad[rows:]
         c_copy(t).start()
+
+    def query_step(g):
+        grad = jnp.dot(pt[...], wts[:, g * 256:(g + 1) * 256], preferred_element_type=f32)
+        for half in range(2):
+            slot = 2 * g + half
+            piece = grad[:, half * rows:(half + 1) * rows]
+            if slot < AXIS:
+                qown[slot] = piece
+            for way in range(2):
+                d, e = DXY[slot] if way == 0 else DXY[slot][::-1]
+                if d > 0:
+                    k = 16 * way + 4 * d + e
+                    gsend[k], gstep[k] = quantized(piece[way * rows:(way + 1) * rows])
+                    for copy in g_copies(way, d, e):
+                        copy.start()
+
+    first = (7, 5, 6)
+    later = (1, 2, 3, 4, 0)
+    for t in first:
+        for g in range(chunks):
+            set_weights(t, g)
+        poi_step(t)
+        if t != first[0]:
+            combine(first[first.index(t) - 1])
+    waiting = [first[-1]]
+    for g in range(chunks - 1, -1, -1):
+        for t in later:
+            set_weights(t, g)
+        query_step(g)
+        if waiting:
+            combine(waiting.pop(0))
+    for number, t in enumerate(later):
+        poi_step(t)
         if number >= LAG:
-            combine(order[number - LAG])
-    for t in order[NZ - LAG:]:
+            combine(later[number - LAG])
+    for t in later[len(later) - LAG:]:
         combine(t)
 
     def decoded(v, step):
         return v.astype(jnp.int32).astype(f32) * step
 
+    def add_line(way, e):
+        mine = qown[line(1 - way, e), way * rows:(way + 1) * rows]
+        for d in (1, 3, 2):
+            for copy in g_copies(way, (4 - d) % 4, e):
+                copy.wait_recv()
+            k = 16 * way + 4 * d + e
+            mine += decoded(grecv[k], gstepr[k])
+        return mine
+
+    def pass_line(way, e):
+        k = 4 * way + e
+        esend[k], estep[k] = quantized(add_line(way, e))
+        for copy in e_copies(way, e):
+            copy.start()
+
+    pass_line(0, 2)
+    pass_line(1, 2)
     for side_no, t in enumerate((3, 4)):
         z_arrived(5 + side_no)
         z_arrived(7 + side_no)
@@ -370,15 +431,22 @@
         zsend[t], zstep[t] = quantized(jnp.concatenate(halves, axis=0))
         z_send(t)
 
+    for e in (1, 3):
+        pass_line(0, e)
+        pass_line(1, e)
+
     found = jnp.sum(ps[:, :rows], axis=0, keepdims=True)
-    grads = qown[...]
-    for slot in range(PLANE - 1, 0, -1):
-        g_copy(BACK[slot]).wait_recv()
+    for slot in range(1, PLANE):
         s_copy(BACK[slot]).wait_recv()
-        found += sidr[slot, 0:1]
-        grads += decoded(qrecv[slot], sidr[slot, 1:2])
+        found += sidr[slot]
     loss_ref[...] = lsum - found * scale
-    qg_ref[...] = grads
+    for way in range(2):
+        grads = add_line(way, 0)
+        for d in (2, 1, 3):
+            for copy in e_copies(way, (4 - d) % 4):
+                copy.wait_recv()
+            grads += decoded(erecv[4 * way + d], estepr[4 * way + d])
+        qg_ref[way * rows:(way + 1) * rows, :] = grads
 
     grads = own[0]
     for t in range(1, 5):
@@ -397,7 +465,13 @@
     for slot in range(1, PLANE):
         n_copy(slot).wait_send()
         s_copy(slot).wait_send()
-        g_copy(slot).wait_send()
+    for way in range(2):
+        for d in range(1, 4):
+            for copy in e_copies(way, d):
+                copy.wait_send()
+            for e in range(4):
+                for copy in g_copies(way, d, e):
+                    copy.wait_send()
     for slot in range(1, AXIS):
         q_copy(slot).wait_send()
         for copy in pass_on(slot):
@@ -417,6 +491,7 @@
     nq = PLANE * rows
     npoi = 2 * NZ * rows
     vmem = pl.BlockSpec(memory_space=pltpu.VMEM)
+    hbm = pl.BlockSpec(memory_space=pl.ANY)
     dma = pltpu.SemaphoreType.DMA
     loss, query_grad, poi_grad = pl.pallas_call(
         kernel,
@@ -425,9 +500,13 @@
             jax.ShapeDtypeStruct((width, rows), f32),
             jax.ShapeDtypeStruct((rows, width), f32),
         ),
-        in_specs=[vmem, vmem, vmem, vmem, pl.BlockSpec(memory_space=pltpu.SMEM), vmem],
+        in_specs=[hbm, hbm, hbm, hbm, pl.BlockSpec(memory_space=pltpu.SMEM), hbm],
         out_specs=(vmem, vmem, vmem),
         scratch_shapes=[
+            pltpu.VMEM((1, rows), jnp.int32),
+            pltpu.VMEM((1, rows), jnp.int32),
+            pltpu.VMEM((regions, regions), jnp.int32),
+            dma((5,)),
             pltpu.VMEM((PLANE, EXT, width), bf16),
             pltpu.VMEM((2 * NZ, EXT, width), bf16),
             pltpu.VMEM((width, npoi), bf16),
@@ -442,8 +521,8 @@
             pltpu.VMEM((8, nq), f32),
             pltpu.VMEM((1, nq), f32),
             pltpu.VMEM((PLANE, 1, nq), f32),
-            pltpu.VMEM((PLANE, 8, rows), f32),
-            pltpu.VMEM((PLANE, 8, rows), f32),
+            pltpu.VMEM((PLANE, 1, rows), f32),
+            pltpu.VMEM((PLANE, 1, rows), f32),
             pltpu.VMEM((NZ, rows, width), f32),
             pltpu.VMEM((NZ, rows, width), f32),
             pltpu.VMEM((NZ, rows, width), f32),
@@ -453,13 +532,19 @@
             pltpu.VMEM((2, HALF, width), jnp.int16),
             pltpu.VMEM((NZ + 1, 1, width), f32),
             pltpu.VMEM((NZ + 1, 1, width), f32),
-            pltpu.VMEM((width, rows), f32),
-            pltpu.VMEM((PLANE, width, rows), jnp.int16),
-            pltpu.VMEM((PLANE, width, rows), jnp.int16),
+            pltpu.VMEM((AXIS, width, rows), f32),
+            pltpu.VMEM((32, width // 2, rows), jnp.int16),
+            pltpu.VMEM((32, width // 2, rows), jnp.int16),
+            pltpu.VMEM((32, 1, rows), f32),
+            pltpu.VMEM((32, 1, rows), f32),
+            pltpu.VMEM((8, width // 2, rows), jnp.int16),
+            pltpu.VMEM((8, width // 2, rows), jnp.int16),
+            pltpu.VMEM((8, 1, rows), f32),
+            pltpu.VMEM((8, 1, rows), f32),
             dma((PLANE,)), dma((PLANE,)), dma((2 * PLANE,)), dma((2 * PLANE,)), dma((NZ + 1,)), dma((NZ + 1,)),
             dma((NZ,)), dma((NZ,)), dma((PLANE,)), dma((PLANE,)), dma((PLANE,)), dma((PLANE,)),
             dma((NZ,)), dma((NZ,)), dma((NZ + 1,)), dma((NZ + 1,)), dma((NZ + 1,)), dma((NZ + 1,)),
-            dma((PLANE,)), dma((PLANE,)),
+            dma((32,)), dma((32,)), dma((32,)), dma((32,)), dma((8,)), dma((8,)), dma((8,)), dma((8,)),
         ],
         compiler_params=pltpu.CompilerParams(
             collective_id=0, has_side_effects=True, vmem_limit_bytes=56 * 2**20

time: 56.2 us -> 56.6 us (level)
  no operation moved by 1% of the time
where the time goes in v5:
time: 56.6 us; the launch traced here: 56.5 us
  Pallas kernels  55.2 us (98%)
  between operations  1.29 us (2%)
    pallas_call x1, Pallas kernels, body(): pl.pallas_call(kernel, out_shape=(jax.ShapeDtypeStruct((1, rows), f32), j...  53.4 us
    pallas_call x1, Pallas kernels, body(): pl.pallas_call(finish, out_shape=(jax.ShapeDtypeStruct((1, rows), f32), j...  1.77 us

profile of v5, /device:TPU:1, one launch (start us, length us, event | category | flops | bytes accessed | tf_op | source)
XLA Modules:
  0.0 56.5 jit_solution(6789088152644569470)
XLA Ops:
  1.3 53.4 %shard_map.85 = (f32[1,128]{1,0:T(1,128)}, f32[256,128]{1,0:T(8,128)}, f32[128,256]{1,0:T(8,128)}) custom-call(bf16[128,256]{1,0:T(8,128)(2,1)} %q_ref.1, bf16[128,256]{1,0:T(8,128)(2,1)} %p_ref.1, s32[1,128]{1,0:T(1,128)} %bitcast.3, s32[1,128]{1,0:T(1,128)} %bitcast.4, s32[1]{0:T(128)S(6)} %copy.9.breg_ref, s32[64,64]{1,0:T(8,128)} %mask_ref.1), custom_call_target="tpu_custom_call" | custom-call | tf_op jit(solution)/shard_map/pallas_call | solution.py:496
  54.7 1.8 %shard_map.86 = (f32[1,128]{1,0:T(1,128)}, f32[128,256]{1,0:T(8,128)}, f32[128,256]{1,0:T(8,128)}) custom-call(f32[1,128]{1,0:T(1,128)} %get-tuple-element.9.loss_ref, f32[256,128]{1,0:T(8,128)} %get-tuple-element.10.qt_ref, f32[128,256]{1,0:T(8,128)} %get-tuple-element.11.pg_ref), custom_call_target="tpu_custom_call" | custom-call | tf_op jit(solution)/shard_map/pallas_call | solution.py:555

commit v6 on v5

--- a/solution.py
+++ b/solution.py
@@ -379,21 +379,28 @@
                     for copy in g_copies(way, d, e):
                         copy.start()
 
-    first = (7, 5, 6)
     later = (1, 2, 3, 4, 0)
-    for t in first:
+
+    def early(t):
         for g in range(chunks):
             set_weights(t, g)
         poi_step(t)
-        if t != first[0]:
-            combine(first[first.index(t) - 1])
-    waiting = [first[-1]]
-    for g in range(chunks - 1, -1, -1):
+
+    def chunk(g):
         for t in later:
             set_weights(t, g)
         query_step(g)
-        if waiting:
-            combine(waiting.pop(0))
+
+    early(7)
+    early(5)
+    early(6)
+    chunk(7)
+    combine(7)
+    combine(5)
+    chunk(6)
+    combine(6)
+    for g in range(chunks - 3, -1, -1):
+        chunk(g)
     for number, t in enumerate(later):
         poi_step(t)
         if number >= LAG:
@@ -419,8 +426,6 @@
         for copy in e_copies(way, e):
             copy.start()
 
-    pass_line(0, 2)
-    pass_line(1, 2)
     for side_no, t in enumerate((3, 4)):
         z_arrived(5 + side_no)
         z_arrived(7 + side_no)
@@ -431,7 +436,7 @@
         zsend[t], zstep[t] = quantized(jnp.concatenate(halves, axis=0))
         z_send(t)
 
-    for e in (1, 3):
+    for e in (2, 1, 3):
         pass_line(0, e)
         pass_line(1, e)
 

time: 56.6 us -> 54.8 us (0.968)
  Pallas kernels: 55.2 us -> 53.3 us
    pallas_call x1, Pallas kernels: 53.4 us -> 51.6 us  [body(): pl.pallas_call(kernel, out_shape=(jax.ShapeDtypeStruct((1, rows), f32), j...]
where the time goes in v6:
time: 54.8 us; the launch traced here: 54.6 us
  Pallas kernels  53.3 us (97%)
  between operations  1.29 us (2%)
    pallas_call x1, Pallas kernels, body(): pl.pallas_call(kernel, out_shape=(jax.ShapeDtypeStruct((1, rows), f32), j...  51.6 us
    pallas_call x1, Pallas kernels, body(): pl.pallas_call(finish, out_shape=(jax.ShapeDtypeStruct((1, rows), f32), j...  1.77 us

profile of v6, /device:TPU:1, one launch (start us, length us, event | category | flops | bytes accessed | tf_op | source)
XLA Modules:
  0.0 54.6 jit_solution(13006729247014283478)
XLA Ops:
  1.3 51.6 %shard_map.85 = (f32[1,128]{1,0:T(1,128)}, f32[256,128]{1,0:T(8,128)}, f32[128,256]{1,0:T(8,128)}) custom-call(bf16[128,256]{1,0:T(8,128)(2,1)} %q_ref.1, bf16[128,256]{1,0:T(8,128)(2,1)} %p_ref.1, s32[1,128]{1,0:T(1,128)} %bitcast.3, s32[1,128]{1,0:T(1,128)} %bitcast.4, s32[1]{0:T(128)S(6)} %copy.9.breg_ref, s32[64,64]{1,0:T(8,128)} %mask_ref.1), custom_call_target="tpu_custom_call" | custom-call | tf_op jit(solution)/shard_map/pallas_call | solution.py:501
  52.9 1.8 %shard_map.86 = (f32[1,128]{1,0:T(1,128)}, f32[128,256]{1,0:T(8,128)}, f32[128,256]{1,0:T(8,128)}) custom-call(f32[1,128]{1,0:T(1,128)} %get-tuple-element.9.loss_ref, f32[256,128]{1,0:T(8,128)} %get-tuple-element.10.qt_ref, f32[128,256]{1,0:T(8,128)} %get-tuple-element.11.pg_ref), custom_call_target="tpu_custom_call" | custom-call | tf_op jit(solution)/shard_map/pallas_call | solution.py:560

commit v7 on v6

--- a/solution.py
+++ b/solution.py
@@ -379,7 +379,7 @@
                     for copy in g_copies(way, d, e):
                         copy.start()
 
-    later = (1, 2, 3, 4, 0)
+    later = (1, 3, 4, 2, 0)
 
     def early(t):
         for g in range(chunks):
@@ -405,8 +405,7 @@
         poi_step(t)
         if number >= LAG:
             combine(later[number - LAG])
-    for t in later[len(later) - LAG:]:
-        combine(t)
+    combine(2)
 
     def decoded(v, step):
         return v.astype(jnp.int32).astype(f32) * step
@@ -436,6 +435,7 @@
         zsend[t], zstep[t] = quantized(jnp.concatenate(halves, axis=0))
         z_send(t)
 
+    combine(0)
     for e in (2, 1, 3):
         pass_line(0, e)
         pass_line(1, e)

time: 54.8 us -> 54.5 us (level)
  no operation moved by 1% of the time
where the time goes in v7:
time: 54.5 us; the launch traced here: 54.3 us
  Pallas kernels  53 us (97%)
  between operations  1.29 us (2%)
    pallas_call x1, Pallas kernels, body(): pl.pallas_call(kernel, out_shape=(jax.ShapeDtypeStruct((1, rows), f32), j...  51.3 us
    pallas_call x1, Pallas kernels, body(): pl.pallas_call(finish, out_shape=(jax.ShapeDtypeStruct((1, rows), f32), j...  1.77 us

profile of v7, /device:TPU:1, one launch (start us, length us, event | category | flops | bytes accessed | tf_op | source)
XLA Modules:
  0.0 54.3 jit_solution(6416321424707680725)
XLA Ops:
  1.3 51.3 %shard_map.85 = (f32[1,128]{1,0:T(1,128)}, f32[256,128]{1,0:T(8,128)}, f32[128,256]{1,0:T(8,128)}) custom-call(bf16[128,256]{1,0:T(8,128)(2,1)} %q_ref.1, bf16[128,256]{1,0:T(8,128)(2,1)} %p_ref.1, s32[1,128]{1,0:T(1,128)} %bitcast.3, s32[1,128]{1,0:T(1,128)} %bitcast.4, s32[1]{0:T(128)S(6)} %copy.9.breg_ref, s32[64,64]{1,0:T(8,128)} %mask_ref.1), custom_call_target="tpu_custom_call" | custom-call | tf_op jit(solution)/shard_map/pallas_call | solution.py:501
  52.6 1.8 %shard_map.86 = (f32[1,128]{1,0:T(1,128)}, f32[128,256]{1,0:T(8,128)}, f32[128,256]{1,0:T(8,128)}) custom-call(f32[1,128]{1,0:T(1,128)} %get-tuple-element.9.loss_ref, f32[256,128]{1,0:T(8,128)} %get-tuple-element.10.qt_ref, f32[128,256]{1,0:T(8,128)} %get-tuple-element.11.pg_ref), custom_call_target="tpu_custom_call" | custom-call | tf_op jit(solution)/shard_map/pallas_call | solution.py:560
